TPU v7x, 32 devices: a whole 2x2x4 slice. The times are simulated.
32 devices in a mesh: event: 8 (over z, core), mesh: 4 (over y, x).
Axes of the slice: x: 2, y: 2, z: 4, core: 2. Of those that a mesh axis runs over, the one named last changes fastest.
Arguments:
- forward_start: float32 [8, 3, 125, 512], P('event', None, None, 'mesh'), may hold values from -6 to 6
- adjoint_start: float32 [8, 3, 125, 512], P('event', None, None, 'mesh'), may hold values from -6 to 6
- stiffness: float32 [125, 125], replicated
- projection: float32 [125, 64], replicated, may hold values from -0.5 to 0.5
- material: float32 [8, 512], P('event', 'mesh'), may hold values from 0.5 to 2
- neighbours: int32 [8, 6, 512], P('event', None, 'mesh'), may hold values from 0 to 511, as said below
- destinations: int32 [8, 512], P('event', 'mesh'), may hold values from 0 to 127
- counts: int32 [8, 4], P('event', 'mesh'), may hold values from 32 to 128, as said below
- smoothing: float32 [4, 128], P(None, ('event', 'mesh')), may hold values from 0.02 to 0.12
Outputs:
- forward_final: float32 [8, 3, 125, 512], P('event', None, None, 'mesh')
- tiles: float32 [64, 128], P(None, ('event', 'mesh'))
Inputs may be any that keep to these rules, and one draw needn't show every extreme that they name: `counts`: in every event one partition holds exactly 128 live elements and another exactly 32; live elements fill a partition's first slots. `neighbours`: A neighbour slot lies in the element's own partition, or in the previous or next partition of the same event (wrapping around), and then among that partition's first 32 slots.
All inputs are finite; a program needn't handle non-finite values.
Results may differ from a plain program's by a relative error of at most 0.0003.
Values sent between devices are 32-bit elements; how exact they have to be, the bound alone decides.
A program may use at most 64 MiB of HBM per device.

v0:
```python
import functools
import math

import jax
import jax.numpy as jnp
from jax import lax
from jax.experimental import pallas as pl
from jax.experimental.pallas import tpu as pltpu
from jax.sharding import PartitionSpec as P

STEPS = 2
time_square = 0.4
penalty = 0.5

PAD = 8
ROWS = 128
NODES = 125
SHIFT = (100, -100, 20, -20, 4, -4)
MESH = pl.DeviceIdType.MESH
f32 = jnp.float32
bf16 = jnp.bfloat16


def on_face(face, node):
    i, j, k = node // 25, (node // 5) % 5, node % 5
    return (i == 0, i == 4, j == 0, j == 4, k == 0, k == 4)[face]


TILE_FACES = [
    [f for f in range(6) if any(on_face(f, n) for n in range(8 * t, min(8 * t + 8, NODES)))]
    for t in range(ROWS // 8)
]


def split(x):
    high = x.astype(bf16)
    return high, (x - high.astype(f32)).astype(bf16)


def mm(a, b, dims=((1,), (0,))):
    return lax.dot_general(a, b, (dims, ((), ())), preferred_element_type=f32)


def pick(x, index):
    return jnp.take_along_axis(x, index, axis=1, mode="promise_in_bounds")


def kernel(
    m_size, e_size,
    fwd_in, adj_in, stiff_hbm, proj_hbm, mat_hbm, nb_hbm, dest_hbm, count_hbm, smooth_hbm,
    fwd_out, tiles_out,
    stiff_in, proj_in, mat_in, nb_in, dest_in, count_in, smooth_in,
    F, N, K, S, W, IDX, LIVE, send, rim, rim2, coef, coef_in, msg, part, got, mine, got2,
    in_s, small_s, out_s, rim_s, rim_r, rim2_s, rim2_r, coef_s, coef_r, a_s, a_r, b_s, b_r, rounds,
):
    me = lax.axis_index("mesh")
    ev = lax.axis_index("event")
    total = m_size * e_size
    lin = ev * m_size + me
    after = lax.rem(me + 1, m_size)
    before = lax.rem(me + m_size - 1, m_size)

    barrier = pltpu.get_barrier_semaphore()
    core = lax.rem(ev, 2)
    chip = lax.div(ev, 2)
    chips = e_size // 2
    near = [((2 * chip + 1 - core, me), None)]
    for step in (1, -1):
        inside = (chip + step >= 0) & (chip + step < chips)
        near += [((2 * (chip + step) + c, me), inside) for c in range(2)]
    near_count = 1 + 2 * ((chip > 0).astype(jnp.int32) + (chip < chips - 1).astype(jnp.int32))

    def greet(sem):
        for device, inside in near:
            if inside is None:
                pl.semaphore_signal(sem, inc=1, device_id=device, device_id_type=MESH)
            else:

                @pl.when(inside)
                def _():
                    pl.semaphore_signal(sem, inc=1, device_id=device, device_id_type=MESH)

    for o in range(1, m_size):
        pl.semaphore_signal(
            barrier, inc=1, device_id=(ev, lax.rem(me + o, m_size)), device_id_type=MESH
        )
    greet(barrier)

    loads = []
    for fc in range(6):
        source = fwd_in if fc < 3 else adj_in
        load = pltpu.make_async_copy(
            source.at[pl.ds(NODES * (fc % 3), NODES), 0], F.at[fc, pl.ds(PAD, NODES)], in_s.at[fc]
        )
        load.start()
        loads.append(load)

    small = []
    for n, (src, dst) in enumerate((
        (smooth_hbm, smooth_in), (stiff_hbm, stiff_in), (nb_hbm, nb_in), (count_hbm, count_in),
        (mat_hbm, mat_in), (proj_hbm, proj_in), (dest_hbm, dest_in),
    )):
        load = pltpu.make_async_copy(src, dst, small_s.at[n])
        load.start()
        small.append(load)

    lane = lax.broadcasted_iota(jnp.int32, (1, 128), 1)
    zero8 = jnp.zeros((PAD, 128), f32)
    for fc in range(6):
        F[fc, 0:PAD, :] = zero8
        F[fc, PAD + NODES : 144, :] = jnp.zeros((144 - PAD - NODES, 128), f32)

    def pack(base):
        wide = [F[base + c, PAD : PAD + ROWS, :] for c in range(3)]
        head = jnp.where(
            lane < 32,
            wide[0][:96],
            jnp.where(lane < 64, pltpu.roll(wide[1][:96], 32, 1), pltpu.roll(wide[2][:96], 64, 1)),
        )
        tail = pltpu.roll(jnp.concatenate([w[96:] for w in wide], axis=0), 96, 1)
        return jnp.where(lane < 96, head, tail)

    for f in range(2):
        for load in loads[3 * f : 3 * f + 3]:
            load.wait()
        send[f] = pack(3 * f)
    coef[...] = jnp.zeros((8, 128), f32)
    small[0].wait()
    coef[0:4, 0:4] = smooth_in[...]

    pl.semaphore_wait(barrier, near_count + (m_size - 1))

    def remote(src, dst, s, r, device):
        copy = pltpu.make_async_remote_copy(
            src_ref=src, dst_ref=dst, send_sem=s, recv_sem=r, device_id=device, device_id_type=MESH
        )
        copy.start()
        return copy

    paired = m_size == 4
    first = 1 - lax.rem(me, 2) if paired else 0
    second = 1 - first
    rows = pl.ds(PAD, 96)

    def to_sides(src, land, sends, recvs):
        slots = (second, first) if paired else (first, second)
        return [
            remote(src, land.at[slot, rows], sends.at[n], recvs.at[n],
                   (ev, jnp.where(slot == 0, after, before)))
            for n, slot in enumerate(slots)
        ]

    rim_copies = [
        to_sides(send.at[0], rim.at[0], rim_s.at[0], rim_r.at[0]),
        to_sides(send.at[1], rim.at[1], rim_s.at[1], rim_r.at[1]),
    ]
    coef_copies = [
        remote(coef, coef_in.at[0], coef_s.at[0], coef_r.at[0], (ev, after)),
        remote(coef, coef_in.at[1], coef_s.at[1], coef_r.at[1], (ev, before)),
    ]
    if chips > 2:
        greet(rounds.at[0])

    for load in small[1:]:
        load.wait()
    live = jnp.where(lane < count_in[0:1, 0:1], 1.0, 0.0).astype(f32)
    LIVE[...] = jnp.broadcast_to(live, (8, 128))
    for fc in range(6):
        F[fc, PAD : PAD + NODES, :] = F[fc, PAD : PAD + NODES, :] * live

    node = lax.broadcasted_iota(jnp.int32, (ROWS, 128), 0).astype(f32)
    i = jnp.floor((node + 0.5) / 25.0)
    rest = node - 25.0 * i
    j = jnp.floor((rest + 0.5) / 5.0)
    k = rest - 5.0 * j
    count = jnp.zeros((ROWS, 128), f32)
    for f, test in enumerate((i == 0.0, i == 4.0, j == 0.0, j == 4.0, k == 0.0, k == 4.0)):
        mask = jnp.where(test & (node < NODES - 0.5), 1.0, 0.0).astype(f32)
        W[f] = mask
        count = count + mask
    W[6] = count
    nb = nb_in[:, 0, :]
    target = lax.shift_right_logical(nb, 7)
    slot = nb & 127
    relative = lax.rem(target - me + m_size, m_size)
    for f in range(6):
        IDX[f] = jnp.broadcast_to(slot[f : f + 1], (8, 128))
        IDX[6 + f] = jnp.broadcast_to(relative[f : f + 1], (8, 128))
    S[...] = jnp.zeros((ROWS, ROWS), f32)
    S[0:NODES, 0:NODES] = stiff_in[...]
    s_hi, s_lo = split(S[...])
    material = mat_in[...]

    def strain(base):
        wide = jnp.concatenate([F[base + c, PAD : PAD + ROWS, :] for c in range(3)], axis=1)
        hi, lo = split(wide)
        both = mm(s_hi, hi) + (mm(s_hi, lo) + mm(s_lo, hi))
        return [both[:, 128 * c : 128 * (c + 1)] for c in range(3)]

    def face_sums(read, offset, relative_to):
        sums = [None] * (ROWS // 8)
        for f in range(6):
            at = IDX[f] if offset is None else (IDX[f] & 31) + offset
            here = IDX[6 + f] == relative_to
            for t in range(ROWS // 8):
                if f in TILE_FACES[t]:
                    g = jnp.where(here, pick(read(8 * t + PAD + SHIFT[f]), at), 0.0)
                    g = g * W[f, 8 * t : 8 * t + 8, :]
                    sums[t] = g if sums[t] is None else sums[t] + g
        return sums

    def own_pass(base):
        def body(c, carry):
            sums = face_sums(lambda low: F[base + c, low : low + 8, :], None, 0)
            for t in range(ROWS // 8):
                at = pl.ds(8 * t, 8)
                v = F[base + c, 8 * t + PAD : 8 * t + 2 * PAD, :]
                acc = sums[t] - W[6, at, :] * v
                N[base + c, at, :] = N[base + c, at, :] + (time_square * penalty) * acc
            return carry

        lax.fori_loop(0, 3, body, 0)

    def unpack(ref):
        pieces = [
            pltpu.roll(ref[PAD + 32 * c : PAD + 32 * c + 32, :], 32 * (c + 1), 1) for c in range(3)
        ]
        ref[PAD + 96 : PAD + 128, :] = jnp.where(
            lane < 32, pieces[0], jnp.where(lane < 64, pieces[1], pieces[2])
        )
        ref[0:PAD, :] = zero8
        ref[PAD + 128 : PAD + 136, :] = zero8

    def rim_pass(base, ref, side, store):
        relative_to = jnp.where(side == 1, 1, m_size - 1)

        def body(c, carry):
            sums = face_sums(lambda low: ref[low : low + 8, :], 32 * c, relative_to)
            for t in range(ROWS // 8):
                old = N[base + c, 8 * t : 8 * t + 8, :]
                store(c, t, old + (time_square * penalty) * sums[t])
            return carry

        lax.fori_loop(0, 3, body, 0)

    def add(base):
        def store(c, t, value):
            N[base + c, 8 * t : 8 * t + 8, :] = value

        return store

    st_f = strain(0)
    st_a = strain(3)
    energy = jnp.zeros((ROWS, 128), f32)
    for c in range(3):
        vf = F[c, PAD : PAD + ROWS, :]
        energy = energy + vf * st_a[c]
        N[c] = vf - time_square * material * st_f[c]
        N[3 + c] = F[3 + c, PAD : PAD + ROWS, :] - time_square * material * st_a[c]
    K[...] = energy
    own_pass(0)
    for n in range(chips - 2):
        pl.semaphore_wait(rounds.at[n], near_count)
        if n + 1 < chips - 2:
            greet(rounds.at[n + 1])
        if n == 0:
            own_pass(3)
    if chips <= 2:
        own_pass(3)

    def keep(base):
        def store(c, t, value):
            value = LIVE[...] * value
            at = pl.ds(8 * t + PAD, 8)
            if base == 0:
                N[c, 8 * t : 8 * t + 8, :] = 2.0 * value - F[c, at, :]
            F[base + c, at, :] = value

        return store

    for f in range(2):
        rim_copies[f][0].wait_recv()
        near_ref = rim.at[f, first]
        unpack(near_ref)
        rim_pass(3 * f, near_ref, first, add(3 * f))
    for f in range(2):
        rim_copies[f][1].wait_recv()
        far_ref = rim.at[f, second]
        unpack(far_ref)
        rim_pass(3 * f, far_ref, second, keep(3 * f))
        if f == 0:
            send[2] = pack(0)

    st_a = strain(3)
    energy = K[...]
    for c in range(3):
        energy = energy + F[c, PAD : PAD + ROWS, :] * st_a[c]
    elements = F.shape[-1]
    width = smooth_in.shape[1]
    scale = math.sqrt(width / elements) / STEPS
    twin = jnp.concatenate([proj_in[...], proj_in[...]], axis=0)
    K[...] = energy
    t_hi, t_lo = split(twin)
    k_hi, k_lo = split(K[0:NODES, :])
    blocks = (mm(t_hi, k_hi) + (mm(t_hi, k_lo) + mm(t_lo, k_hi))) * scale
    b_hi, b_lo = split(blocks)
    row = lax.broadcasted_iota(jnp.int32, (total * width, 128), 0)
    owner = lax.div(row, width)
    tile = width * (lax.rem(owner, e_size) * m_size + lax.div(owner, e_size)) + lax.rem(row, width)
    dest = dest_in[...]
    nt = ((1,), (1,))

    def spread(offset):
        hot = jnp.where(tile + offset == dest, 1.0, 0.0).astype(f32).astype(bf16)
        return mm(hot, b_hi, nt) + mm(hot, b_lo, nt)

    packed = jnp.where(lane < 64, spread(-2), spread(2))
    msg[...] = packed.reshape(m_size, e_size, width, 128)
    a_copies = [
        remote(msg.at[lax.rem(me + o, m_size)], got.at[o - 1], a_s.at[o - 1], a_r.at[o - 1],
               (ev, lax.rem(me + o, m_size)))
        for o in range(1, m_size)
    ]

    rim2_copies = to_sides(send.at[2], rim2, rim2_s, rim2_r)

    st_f = strain(0)
    for c in range(3):
        N[c] = N[c] - time_square * material * st_f[c]
    own_pass(0)

    for copy in coef_copies:
        copy.wait_recv()
    coef_copies += [
        remote(coef_in.at[0], coef_in.at[2], coef_s.at[2], coef_r.at[2],
               (lax.rem(ev + 1, e_size), me)),
        remote(coef_in.at[1], coef_in.at[3], coef_s.at[3], coef_r.at[3],
               (lax.rem(ev + e_size - 1, e_size), me)),
    ]
    for copy in a_copies:
        copy.wait_recv()
    mine_sum = msg[me]
    for o in range(m_size - 1):
        mine_sum = mine_sum + got[o]
    part[...] = mine_sum
    b_copies = [
        remote(part.at[lax.rem(ev + o, e_size)], got2.at[o - 1], b_s.at[o - 1], b_r.at[o - 1],
               (lax.rem(ev + o, e_size), me))
        for o in range(1, e_size)
    ]

    def final(c, t, value):
        N[c, 8 * t : 8 * t + 8, :] = LIVE[...] * value

    for n, side in enumerate((first, second)):
        rim2_copies[n].wait_recv()
        ref = rim2.at[side]
        unpack(ref)
        rim_pass(0, ref, side, add(0) if n == 0 else final)
    stores = []
    for c in range(3):
        store = pltpu.make_async_copy(
            N.at[c, pl.ds(0, NODES)], fwd_out.at[pl.ds(NODES * c, NODES), 0], out_s.at[c]
        )
        store.start()
        stores.append(store)

    for copy in coef_copies[2:]:
        copy.wait_recv()
    own_coef = pltpu.roll(coef[...], 2, 1)
    left = jnp.where(lin > 0, jnp.where(me > 0, coef_in[0], coef_in[2]), 0.0)
    right = jnp.where(
        lin < total - 1, jnp.where(me < m_size - 1, coef_in[1], coef_in[3]), 0.0
    )
    left = jnp.where(lane < 2, pltpu.roll(left, 126, 1), 0.0)
    right = pltpu.roll(right, 6, 1)
    mine[...] = jnp.zeros((128, 128), f32)
    mine[0:8, :] = own_coef + left + right
    coefs = mine[...].T[0:8]

    def smooth(x):
        chain = pltpu.roll(x, 1, 0) + pltpu.roll(x, 7, 0) - 2.0 * x
        new = x + coefs[:, 0:1] * chain
        for d, shift in ((1, 4), (2, 2), (3, 0)):
            digit = lax.shift_right_logical(lane, shift) & 3
            up = jnp.where(digit == 0, 0.0, pltpu.roll(x, 1 << shift, 1))
            down = jnp.where(digit == 3, 0.0, pltpu.roll(x, 128 - (1 << shift), 1))
            new = new + coefs[:, d : d + 1] * (up + down - 2.0 * x)
        return jnp.where(lane < 64, new, 0.0)

    for copy in b_copies:
        copy.wait_recv()
    summed = part[ev]
    for o in range(e_size - 1):
        summed = summed + got2[o]
    x = jnp.concatenate([summed, pltpu.roll(summed, 64, 1)], axis=0)
    x = smooth(smooth(jnp.where(lane < 64, x, 0.0)))
    tiles_out[...] = x[2 : 2 + width, 0:64]

    for store in stores:
        store.wait()
    for copy in rim_copies[0] + rim_copies[1] + rim2_copies + coef_copies + a_copies + b_copies:
        copy.wait_send()


def solution(mesh):
    m_size, e_size = mesh.shape["mesh"], mesh.shape["event"]
    in_specs = (
        P("event", None, None, "mesh"),
        P("event", None, None, "mesh"),
        P(),
        P(),
        P("event", "mesh"),
        P("event", None, "mesh"),
        P("event", "mesh"),
        P("event", "mesh"),
        P(None, ("event", "mesh")),
    )
    out_specs = (P("event", None, None, "mesh"), P(None, ("event", "mesh")))

    def per_device(*args):
        fwd, smoothing = args[0], args[-1]
        width = smoothing.shape[1]
        dma = pltpu.SemaphoreType.DMA
        vmem = pl.BlockSpec(memory_space=pltpu.VMEM)
        hbm = pl.BlockSpec(memory_space=pltpu.HBM)
        line = (3 * NODES, 1, fwd.shape[-1])
        args = (args[0].reshape(line), args[1].reshape(line), args[2], args[3].T, args[4],
                args[5].reshape(6, 1, fwd.shape[-1]), *args[6:])
        final, tiles = pl.pallas_call(
            functools.partial(kernel, m_size, e_size),
            out_shape=(
                pltpu.VMEM(line, f32),
                pltpu.VMEM((width, 64), f32),
            ),
            in_specs=[hbm] * len(args),
            out_specs=(vmem, vmem),
            scratch_shapes=[pltpu.VMEM(x.shape, x.dtype) for x in args[2:]]
            + [
                pltpu.VMEM((6, 144, 128), f32),
                pltpu.VMEM((6, ROWS, 128), f32),
                pltpu.VMEM((ROWS, 128), f32),
                pltpu.VMEM((ROWS, ROWS), f32),
                pltpu.VMEM((7, ROWS, 128), f32),
                pltpu.VMEM((12, 8, 128), jnp.int32),
                pltpu.VMEM((8, 128), f32),
                pltpu.VMEM((3, 96, 128), f32),
                pltpu.VMEM((2, 2, 144, 128), f32),
                pltpu.VMEM((2, 144, 128), f32),
                pltpu.VMEM((8, 128), f32),
                pltpu.VMEM((4, 8, 128), f32),
                pltpu.VMEM((m_size, e_size, width, 128), f32),
                pltpu.VMEM((e_size, width, 128), f32),
                pltpu.VMEM((m_size - 1, e_size, width, 128), f32),
                pltpu.VMEM((128, 128), f32),
                pltpu.VMEM((e_size - 1, width, 128), f32),
                dma((6,)), dma((7,)), dma((3,)), dma((2, 2)), dma((2, 2)), dma((2,)), dma((2,)), dma((4,)), dma((4,)),
                dma((m_size - 1,)), dma((m_size - 1,)), dma((e_size - 1,)), dma((e_size - 1,)),
                pltpu.SemaphoreType.REGULAR((max(e_size // 2 - 2, 1),)),
            ],
            compiler_params=pltpu.CompilerParams(collective_id=0, has_side_effects=True),
        )(*args)
        return final.reshape(fwd.shape), tiles.T

    return jax.shard_map(
        per_device, mesh=mesh, in_specs=in_specs, out_specs=out_specs, check_vma=False
    )
```

profile of v0, /device:TPU:0, one launch (start us, length us, event | category | flops | bytes accessed | tf_op | source)
XLA Modules:
  0.0 23.0 jit_solution(9462650505118679963)
XLA Ops:
  1.3 20.5 %shard_map.104 = (f32[375,1,128]{2,1,0:T(1,128)S(1)}, f32[4,64]{1,0:T(4,128)S(1)}) custom-call(f32[375,1,128]{2,1,0:T(1,128)} %bitcast.8, f32[375,1,128]{2,1,0:T(1,128)} %bitcast.9, f32[125,125]{1,0:T(8,128)} %stiff_hbm.1, f32[64,125]{1,0:T(8,128)} %bitcast.10, f32[1,128]{1,0:T(1,128)} %mat_hbm.1, s32[6,1,128]{2,1,0:T(1,128)} %bitcast.11, ...), custom_call_target="tpu_custom_call" | custom-call | tf_op jit(solution)/shard_map/pallas_call | solution.py:430
  21.8 0.7 %copy.13 = f32[1,3,125,128]{3,0,2,1:T(1,128)} copy(f32[1,3,125,128]{3,0,2,1:T(1,128)S(1)} %bitcast.6) | data formatting | bytes 384000
  22.4 0.6 %copy.14 = f32[64,4]{0,1:T(4,128)} copy(f32[64,4]{0,1:T(4,128)S(1)} %bitcast.7) | data formatting | bytes 2048
where the time goes:
time: 23.2 us; the launch traced here: 23 us
  Pallas kernels  20.5 us (88%)
  between operations  1.29 us (6%)
  local copies, waits for them, and re-layouts  1.26 us (5%)
    pallas_call x1, Pallas kernels, per_device(): pl.pallas_call(functools.partial(kernel, m_size, e_size), out_shape=(pltp...  20.5 us
    unnamed x2, local copies, waits for them, and re-layouts  1.26 us

commit v1 on v0

v1 whole, which is shorter than its diff:
```python
import functools
import math

import jax
import jax.numpy as jnp
from jax import lax
from jax.experimental import pallas as pl
from jax.experimental.pallas import tpu as pltpu
from jax.sharding import PartitionSpec as P

STEPS = 2
time_square = 0.4
penalty = 0.5

PAD = 8
ROWS = 128
NODES = 125
SHIFT = (100, -100, 20, -20, 4, -4)
STRAIGHT_FROM = {1: 2, 0: 1, 2: 2}
MESH = pl.DeviceIdType.MESH
f32 = jnp.float32
bf16 = jnp.bfloat16


def on_face(face, node):
    i, j, k = node // 25, (node // 5) % 5, node % 5
    return (i == 0, i == 4, j == 0, j == 4, k == 0, k == 4)[face]


TILE_FACES = [
    [f for f in range(6) if any(on_face(f, n) for n in range(8 * t, min(8 * t + 8, NODES)))]
    for t in range(ROWS // 8)
]


def split(x):
    high = x.astype(bf16)
    return high, (x - high.astype(f32)).astype(bf16)


def mm(a, b, dims=((1,), (0,))):
    return lax.dot_general(a, b, (dims, ((), ())), preferred_element_type=f32)


def pick(x, index):
    return jnp.take_along_axis(x, index, axis=1, mode="promise_in_bounds")


def is_direct(m_size, e_size):
    return m_size * e_size <= 64


def round_count(m_size, e_size):
    return max(e_size // 2 - 1, 1) if is_direct(m_size, e_size) else max(e_size // 2 - 2, 0)


def kernel(
    m_size, e_size,
    fwd_in, adj_in, stiff_hbm, proj_hbm, mat_hbm, nb_hbm, dest_hbm, count_hbm, smooth_hbm,
    fwd_out, tiles_out,
    stiff_in, proj_in, mat_in, nb_in, dest_in, count_in, smooth_in,
    F, N, K, A, S, W, IDX, RIM, LIVE, send, rim, coef, coef_in, msg, mine, part, got, got2,
    in_s, small_s, rim_s, rim_r, coef_s, coef_r, a_s, a_r, b_s, b_r, rounds,
):
    me = lax.axis_index("mesh")
    ev = lax.axis_index("event")
    total = m_size * e_size
    direct = is_direct(m_size, e_size)
    lin = ev * m_size + me
    after = lax.rem(me + 1, m_size)
    before = lax.rem(me + m_size - 1, m_size)

    barrier = pltpu.get_barrier_semaphore()
    core = lax.rem(ev, 2)
    chip = lax.div(ev, 2)
    chips = e_size // 2
    near = [((2 * chip + 1 - core, me), None)]
    for step in (1, -1):
        inside = (chip + step >= 0) & (chip + step < chips)
        near += [((2 * (chip + step) + c, me), inside) for c in range(2)]
    near_count = 1 + 2 * ((chip > 0).astype(jnp.int32) + (chip < chips - 1).astype(jnp.int32))

    def greet(sem):
        for device, inside in near:
            if inside is None:
                pl.semaphore_signal(sem, inc=1, device_id=device, device_id_type=MESH)
            else:

                @pl.when(inside)
                def _():
                    pl.semaphore_signal(sem, inc=1, device_id=device, device_id_type=MESH)

    for o in range(1, m_size):
        pl.semaphore_signal(
            barrier, inc=1, device_id=(ev, lax.rem(me + o, m_size)), device_id_type=MESH
        )
    greet(barrier)

    loads = {}
    for fc in (3, 4, 5, 0, 1, 2):
        source = fwd_in if fc < 3 else adj_in
        load = pltpu.make_async_copy(
            source.at[pl.ds(NODES * (fc % 3), NODES), 0], F.at[fc, pl.ds(PAD, NODES)], in_s.at[fc]
        )
        load.start()
        loads[fc] = load

    small = []
    for n, (src, dst) in enumerate((
        (smooth_hbm, smooth_in), (stiff_hbm, stiff_in), (nb_hbm, nb_in), (count_hbm, count_in),
        (mat_hbm, mat_in), (proj_hbm, proj_in), (dest_hbm, dest_in),
    )):
        load = pltpu.make_async_copy(src, dst, small_s.at[n])
        load.start()
        small.append(load)

    lane = lax.broadcasted_iota(jnp.int32, (1, 128), 1)
    zero8 = jnp.zeros((PAD, 128), f32)
    for fc in range(6):
        F[fc, 0:PAD, :] = zero8
        F[fc, PAD + NODES : 144, :] = jnp.zeros((144 - PAD - NODES, 128), f32)

    def pack(fc):
        wide = [F[fc, PAD + 32 * g : PAD + 32 * g + 32, :] for g in range(4)]
        turned = [wide[0]] + [pltpu.roll(wide[g], 32 * g, 1) for g in range(1, 4)]
        return jnp.where(
            lane < 64, jnp.where(lane < 32, turned[0], turned[1]),
            jnp.where(lane < 96, turned[2], turned[3]),
        )

    def load_field(f):
        for c in range(3):
            loads[3 * f + c].wait()
            send[f, c] = pack(3 * f + c)

    load_field(1)

    pl.semaphore_wait(barrier, near_count + (m_size - 1))

    def remote(src, dst, s, r, device):
        copy = pltpu.make_async_remote_copy(
            src_ref=src, dst_ref=dst, send_sem=s, recv_sem=r, device_id=device, device_id_type=MESH
        )
        copy.start()
        return copy

    paired = m_size == 4
    first = 1 - lax.rem(me, 2) if paired else 0
    second = 1 - first
    sides = (first, second)
    low32 = pl.ds(0, 32)

    def rim_copy(f, k, c):
        slot = sides[1 - k] if paired else sides[k]
        return pltpu.make_async_remote_copy(
            src_ref=send.at[f, c], dst_ref=rim.at[f, slot, c, low32],
            send_sem=rim_s.at[f, k, c], recv_sem=rim_r.at[f, k, c],
            device_id=(ev, jnp.where(slot == 0, after, before)), device_id_type=MESH,
        )

    def relay_copy(f, c):
        return pltpu.make_async_remote_copy(
            src_ref=rim.at[f, first, c, low32], dst_ref=rim.at[f, second, c, low32],
            send_sem=rim_s.at[f, 1, c], recv_sem=rim_r.at[f, 1, c],
            device_id=(ev, lax.rem(me + 2, m_size)), device_id_type=MESH,
        )

    def straight(f):
        return STRAIGHT_FROM[f] if paired else 0

    def send_near(f):
        for c in range(3):
            rim_copy(f, 0, c).start()

    def send_far(f):
        for c in range(straight(f), 3):
            rim_copy(f, 1, c).start()

    send_near(1)
    load_field(0)
    coef[...] = jnp.zeros((8, 128), f32)
    small[0].wait()
    coef[0:4, 0:4] = smooth_in[...]
    send_far(1)
    coef_copies = [
        remote(coef, coef_in.at[0], coef_s.at[0], coef_r.at[0], (ev, after)),
        remote(coef, coef_in.at[1], coef_s.at[1], coef_r.at[1], (ev, before)),
    ]
    n_rounds = round_count(m_size, e_size)
    if n_rounds:
        greet(rounds.at[0])

    def next_round(n):
        if n < n_rounds:
            pl.semaphore_wait(rounds.at[n], near_count)
            if n + 1 < n_rounds:
                greet(rounds.at[n + 1])

    for load in small[1:]:
        load.wait()
    live = jnp.where(lane < count_in[0:1, 0:1], 1.0, 0.0).astype(f32)
    LIVE[...] = jnp.broadcast_to(live, (8, 128))
    for fc in range(6):
        F[fc, PAD : PAD + NODES, :] = F[fc, PAD : PAD + NODES, :] * live

    node = lax.broadcasted_iota(jnp.int32, (ROWS, 128), 0).astype(f32)
    i = jnp.floor((node + 0.5) / 25.0)
    rest = node - 25.0 * i
    j = jnp.floor((rest + 0.5) / 5.0)
    k = rest - 5.0 * j
    count = jnp.zeros((ROWS, 128), f32)
    for f, test in enumerate((i == 0.0, i == 4.0, j == 0.0, j == 4.0, k == 0.0, k == 4.0)):
        mask = jnp.where(test & (node < NODES - 0.5), 1.0, 0.0).astype(f32)
        W[f] = mask
        count = count + mask
    W[6] = count
    nb = nb_in[:, 0, :]
    target = lax.shift_right_logical(nb, 7)
    slot = nb & 127
    relative = lax.rem(target - me + m_size, m_size)
    for f in range(6):
        IDX[f] = jnp.broadcast_to(slot[f : f + 1], (8, 128))
        IDX[6 + f] = jnp.broadcast_to(relative[f : f + 1], (8, 128))
        for g in range(4):
            RIM[f, g] = jnp.broadcast_to((slot[f : f + 1] & 31) + 32 * g, (8, 128))
    S[...] = jnp.zeros((ROWS, ROWS), f32)
    S[0:NODES, 0:NODES] = stiff_in[...]
    s_hi, s_lo = split(S[...])
    material = mat_in[...]

    def strain(base):
        wide = jnp.concatenate([F[base + c, PAD : PAD + ROWS, :] for c in range(3)], axis=1)
        hi, lo = split(wide)
        both = mm(s_hi, hi) + (mm(s_hi, lo) + mm(s_lo, hi))
        return [both[:, 128 * c : 128 * (c + 1)] for c in range(3)]

    def face_sums(read, relative_to):
        sums = [None] * (ROWS // 8)
        for f in range(6):
            here = IDX[6 + f] == relative_to
            for t in range(ROWS // 8):
                if f in TILE_FACES[t]:
                    g = jnp.where(here, read(f, 8 * t + SHIFT[f]), 0.0)
                    g = g * W[f, 8 * t : 8 * t + 8, :]
                    sums[t] = g if sums[t] is None else sums[t] + g
        return sums

    def own_pass(base):
        def body(c, carry):
            sums = face_sums(lambda f, low: pick(F[base + c, low + PAD : low + 2 * PAD, :], IDX[f]), 0)
            for t in range(ROWS // 8):
                at = pl.ds(8 * t, 8)
                v = F[base + c, 8 * t + PAD : 8 * t + 2 * PAD, :]
                acc = sums[t] - W[6, at, :] * v
                N[base + c, at, :] = N[base + c, at, :] + (time_square * penalty) * acc
            return carry

        lax.fori_loop(0, 3, body, 0)

    def rim_pass(base, f, k, store, after_each=None):
        side = sides[k]
        relative_to = jnp.where(side == 1, 1, m_size - 1)

        def body(c, carry):
            rim_copy(f, k, c).wait_recv()
            if k == 0 and paired and straight(f) > 0:
                if straight(f) == 3:
                    relay_copy(f, c).start()
                else:

                    @pl.when(c < straight(f))
                    def _():
                        relay_copy(f, c).start()

            rim[f, side, c, 32:40, :] = pltpu.roll(rim[f, side, c, 0:8, :], 96, 1)

            def read(face, low):
                at = low % 32
                return pick(rim[f, side, c, at : at + 8, :], RIM[face, (low // 32) % 4])

            sums = face_sums(read, relative_to)
            for t in range(ROWS // 8):
                old = N[base + c, 8 * t : 8 * t + 8, :]
                store(c, t, old + (time_square * penalty) * sums[t])
            if after_each is not None:
                after_each(c)
            return carry

        lax.fori_loop(0, 3, body, 0)

    def send_next(c):
        send[2, c] = pack(c)
        rim_copy(2, 0, c).start()

    def add(base):
        def store(c, t, value):
            N[base + c, 8 * t : 8 * t + 8, :] = value

        return store

    st_f = strain(0)
    st_a = strain(3)
    energy = jnp.zeros((ROWS, 128), f32)
    for c in range(3):
        vf = F[c, PAD : PAD + ROWS, :]
        energy = energy + vf * st_a[c]
        N[c] = vf - time_square * material * st_f[c]
        N[3 + c] = F[3 + c, PAD : PAD + ROWS, :] - time_square * material * st_a[c]
    K[...] = energy
    send_near(0)
    own_pass(3)
    send_far(0)
    own_pass(0)
    next_round(0)

    def keep_adjoint(c, t, value):
        F[3 + c, 8 * t + PAD : 8 * t + 2 * PAD, :] = LIVE[...] * value

    def keep_forward(c, t, value):
        value = LIVE[...] * value
        at = pl.ds(8 * t + PAD, 8)
        line = pl.ds(8 * t, 8)
        N[c, line, :] = 2.0 * value - F[c, at, :]
        F[c, at, :] = value
        K[line, :] = K[line, :] + value * A[c, line, :]

    rim_pass(3, 1, 0, add(3))
    next_round(1)
    rim_pass(0, 0, 0, add(0))
    rim_pass(3, 1, 1, keep_adjoint)
    for n in range(2, n_rounds):
        next_round(n)
    for c, value in enumerate(strain(3)):
        A[c] = value
    rim_pass(0, 0, 1, keep_forward, send_next)

    elements = F.shape[-1]
    width = smooth_in.shape[1]
    scale = math.sqrt(width / elements) / STEPS
    twin = jnp.concatenate([proj_in[...], proj_in[...]], axis=0)
    t_hi, t_lo = split(twin)
    k_hi, k_lo = split(K[0:NODES, :])
    blocks = (mm(t_hi, k_hi) + (mm(t_hi, k_lo) + mm(t_lo, k_hi))) * scale
    b_hi, b_lo = split(blocks)
    row = lax.broadcasted_iota(jnp.int32, (total * width, 128), 0)
    owner = lax.div(row, width)
    tile = width * (lax.rem(owner, e_size) * m_size + lax.div(owner, e_size)) + lax.rem(row, width)
    dest = dest_in[...]
    nt = ((1,), (1,))

    def spread(offset):
        hot = jnp.where(tile + offset == dest, 1.0, 0.0).astype(f32).astype(bf16)
        return mm(hot, b_hi, nt) + mm(hot, b_lo, nt)

    packed = jnp.where(lane < 64, spread(-2), spread(2))
    msg[...] = packed.reshape(m_size, e_size, width, 128)

    def peer(oe, om):
        return lax.rem(ev + oe, e_size), lax.rem(me + om, m_size)

    if direct:
        offsets = [(oe, om) for oe in list(range(1, e_size)) + [0] for om in range(m_size) if oe or om]
        for oe, om in offsets:
            e, m = peer(oe, om)
            remote(msg.at[m, e], got.at[oe * m_size + om - 1], a_s.at[0], a_r.at[0], (e, m))
    else:
        a_copies = [
            remote(msg.at[lax.rem(me + o, m_size)], got.at[pl.ds(e_size * (o - 1), e_size)],
                   a_s.at[o - 1], a_r.at[o - 1], (ev, lax.rem(me + o, m_size)))
            for o in range(1, m_size)
        ]

    send_far(2)

    st_f = strain(0)
    for c in range(3):
        N[c] = N[c] - time_square * material * st_f[c]
    own_pass(0)

    for copy in coef_copies:
        copy.wait_recv()
    coef_copies += [
        remote(coef_in.at[0], coef_in.at[2], coef_s.at[2], coef_r.at[2],
               (lax.rem(ev + 1, e_size), me)),
        remote(coef_in.at[1], coef_in.at[3], coef_s.at[3], coef_r.at[3],
               (lax.rem(ev + e_size - 1, e_size), me)),
    ]
    if not direct:
        for copy in a_copies:
            copy.wait_recv()
        mine_sum = msg[me]
        for o in range(m_size - 1):
            mine_sum = mine_sum + got[e_size * o : e_size * (o + 1)]
        part[...] = mine_sum
        b_copies = [
            remote(part.at[lax.rem(ev + o, e_size)], got2.at[o - 1], b_s.at[o - 1], b_r.at[o - 1],
                   (lax.rem(ev + o, e_size), me))
            for o in range(1, e_size)
        ]

    def final(c, t, value):
        fwd_out[c, 8 * t : 8 * t + 8, :] = LIVE[...] * value

    rim_pass(0, 2, 0, add(0))
    rim_pass(0, 2, 1, final)

    for copy in coef_copies[2:]:
        copy.wait_recv()
    own_coef = pltpu.roll(coef[...], 2, 1)
    left = jnp.where(lin > 0, jnp.where(me > 0, coef_in[0], coef_in[2]), 0.0)
    right = jnp.where(
        lin < total - 1, jnp.where(me < m_size - 1, coef_in[1], coef_in[3]), 0.0
    )
    left = jnp.where(lane < 2, pltpu.roll(left, 126, 1), 0.0)
    right = pltpu.roll(right, 6, 1)
    mine[...] = jnp.zeros((128, 128), f32)
    mine[0:8, :] = own_coef + left + right
    coefs = mine[...].T[0:8]

    def smooth(x):
        chain = pltpu.roll(x, 1, 0) + pltpu.roll(x, 7, 0) - 2.0 * x
        new = x + coefs[:, 0:1] * chain
        for d, shift in ((1, 4), (2, 2), (3, 0)):
            digit = lax.shift_right_logical(lane, shift) & 3
            up = jnp.where(digit == 0, 0.0, pltpu.roll(x, 1 << shift, 1))
            down = jnp.where(digit == 3, 0.0, pltpu.roll(x, 128 - (1 << shift), 1))
            new = new + coefs[:, d : d + 1] * (up + down - 2.0 * x)
        return jnp.where(lane < 64, new, 0.0)

    if direct:
        gathered = pltpu.make_async_remote_copy(
            src_ref=got, dst_ref=got, send_sem=a_s.at[0], recv_sem=a_r.at[0],
            device_id=peer(1, 0), device_id_type=MESH,
        )
        gathered.wait_recv()
        parts = [msg[me, ev]] + [got[n] for n in range(total - 1)]
    else:
        for copy in b_copies:
            copy.wait_recv()
        parts = [part[ev]] + [got2[o] for o in range(e_size - 1)]
    while len(parts) > 1:
        parts = [sum(parts[n : n + 2][1:], parts[n]) for n in range(0, len(parts), 2)]
    summed = parts[0]
    x = jnp.concatenate([summed, pltpu.roll(summed, 64, 1)], axis=0)
    x = smooth(smooth(jnp.where(lane < 64, x, 0.0)))
    tiles_out[...] = x[2 : 2 + width, 0:64]

    for f in range(3):
        for k in range(2):
            for c in range(3):
                rim_copy(f, k, c).wait_send()
    if direct:
        gathered.wait_send()
    else:
        for copy in a_copies + b_copies:
            copy.wait_send()
    for copy in coef_copies:
        copy.wait_send()


def write_out(final_vmem, tiles_vmem, final_hbm, tiles_hbm, sems):
    copies = [
        pltpu.make_async_copy(
            final_vmem.at[c, pl.ds(0, NODES)], final_hbm.at[pl.ds(NODES * c, NODES), 0], sems.at[c]
        )
        for c in range(3)
    ]
    copies.append(pltpu.make_async_copy(tiles_vmem, tiles_hbm, sems.at[3]))
    for copy in copies:
        copy.start()
    for copy in copies:
        copy.wait()


def solution(mesh):
    m_size, e_size = mesh.shape["mesh"], mesh.shape["event"]
    in_specs = (
        P("event", None, None, "mesh"),
        P("event", None, None, "mesh"),
        P(),
        P(),
        P("event", "mesh"),
        P("event", None, "mesh"),
        P("event", "mesh"),
        P("event", "mesh"),
        P(None, ("event", "mesh")),
    )
    out_specs = (P("event", None, None, "mesh"), P(None, ("event", "mesh")))

    def per_device(*args):
        fwd, smoothing = args[0], args[-1]
        width = smoothing.shape[1]
        dma = pltpu.SemaphoreType.DMA
        vmem = pl.BlockSpec(memory_space=pltpu.VMEM)
        hbm = pl.BlockSpec(memory_space=pltpu.HBM)
        line = (3 * NODES, 1, fwd.shape[-1])
        args = (args[0].reshape(line), args[1].reshape(line), args[2], args[3].T, args[4],
                args[5].reshape(6, 1, fwd.shape[-1]), *args[6:])
        if is_direct(m_size, e_size):
            a_count, b_count = 1, 1
            part, got, got2 = (1, width, 128), (m_size * e_size - 1, width, 128), (1, width, 128)
        else:
            a_count, b_count = m_size - 1, e_size - 1
            part, got, got2 = (e_size, width, 128), ((m_size - 1) * e_size, width, 128), (e_size - 1, width, 128)
        final, tiles = pl.pallas_call(
            functools.partial(kernel, m_size, e_size),
            out_shape=(
                pltpu.VMEM((3, ROWS, 128), f32),
                pltpu.VMEM((width, 64), f32),
            ),
            in_specs=[hbm] * len(args),
            out_specs=(vmem, vmem),
            scratch_shapes=[pltpu.VMEM(x.shape, x.dtype) for x in args[2:]]
            + [
                pltpu.VMEM((6, 144, 128), f32),
                pltpu.VMEM((6, ROWS, 128), f32),
                pltpu.VMEM((ROWS, 128), f32),
                pltpu.VMEM((3, ROWS, 128), f32),
                pltpu.VMEM((ROWS, ROWS), f32),
                pltpu.VMEM((7, ROWS, 128), f32),
                pltpu.VMEM((12, 8, 128), jnp.int32),
                pltpu.VMEM((6, 4, 8, 128), jnp.int32),
                pltpu.VMEM((8, 128), f32),
                pltpu.VMEM((3, 3, 32, 128), f32),
                pltpu.VMEM((3, 2, 3, 40, 128), f32),
                pltpu.VMEM((8, 128), f32),
                pltpu.VMEM((4, 8, 128), f32),
                pltpu.VMEM((m_size, e_size, width, 128), f32),
                pltpu.VMEM((128, 128), f32),
                pltpu.VMEM(part, f32),
                pltpu.VMEM(got, f32),
                pltpu.VMEM(got2, f32),
                dma((6,)), dma((7,)), dma((3, 2, 3)), dma((3, 2, 3)), dma((4,)), dma((4,)),
                dma((a_count,)), dma((a_count,)), dma((b_count,)), dma((b_count,)),
                pltpu.SemaphoreType.REGULAR((max(round_count(m_size, e_size), 1),)),
            ],
            compiler_params=pltpu.CompilerParams(collective_id=0, has_side_effects=True),
        )(*args)
        final, tiles = pl.pallas_call(
            write_out,
            out_shape=(pltpu.HBM(line, f32), pltpu.HBM((width, 64), f32)),
            in_specs=[vmem, vmem],
            out_specs=(hbm, hbm),
            scratch_shapes=[dma((4,))],
        )(
            pltpu.with_memory_space_constraint(final, pltpu.VMEM),
            pltpu.with_memory_space_constraint(tiles, pltpu.VMEM),
        )
        return final.reshape(fwd.shape), tiles.T

    return jax.shard_map(
        per_device, mesh=mesh, in_specs=in_specs, out_specs=out_specs, check_vma=False
    )
```

time: 23.2 us -> 21 us (0.905)
  local copies, waits for them, and re-layouts: 1.26 us -> 0 us
  Pallas kernels: 20.5 us -> 19.6 us
    pallas_call x1, Pallas kernels: 20.5 us -> 18.9 us  [per_device(): pl.pallas_call(functools.partial(kernel, m_size, e_size), out_shape=(pltp...]
    unnamed x2 -> x0, local copies, waits for them, and re-layouts: 1.26 us -> none
    pallas_call x0 -> x1, Pallas kernels: none -> 0.71 us  [per_device(): pl.pallas_call(write_out, out_shape=(pltpu.HBM(line, f32), pltpu.HBM((wid...]
where the time goes in v1:
time: 21 us; the launch traced here: 20.9 us
  Pallas kernels  19.6 us (93%)
  between operations  1.29 us (6%)
    pallas_call x1, Pallas kernels, per_device(): pl.pallas_call(functools.partial(kernel, m_size, e_size), out_shape=(pltp...  18.9 us
    pallas_call x1, Pallas kernels, per_device(): pl.pallas_call(write_out, out_shape=(pltpu.HBM(line, f32), pltpu.HBM((wid...  0.71 us

profile of v1, /device:TPU:0, one launch (start us, length us, event | category | flops | bytes accessed | tf_op | source)
XLA Modules:
  0.0 20.9 jit_solution(13669137042626383314)
XLA Ops:
  1.3 18.9 %shard_map.104 = (f32[3,128,128]{2,1,0:T(8,128)S(1)}, f32[4,64]{1,0:T(4,128)S(1)}) custom-call(f32[375,1,128]{2,1,0:T(1,128)} %bitcast.6, f32[375,1,128]{2,1,0:T(1,128)} %bitcast.7, f32[125,125]{1,0:T(8,128)} %stiff_hbm.1, f32[64,125]{1,0:T(8,128)} %bitcast.8, f32[1,128]{1,0:T(1,128)} %mat_hbm.1, s32[6,1,128]{2,1,0:T(1,128)} %bitcast.9, s32[1,128]{1,0:T(1,128)} %dest_hbm.1, ...), custom_call_target="tpu_custom_call" | custom-call | tf_op jit(solution)/shard_map/pallas_call | solution.py:505
  20.1 0.7 %shard_map.105 = (f32[375,1,128]{2,1,0:T(1,128)}, f32[4,64]{1,0:T(4,128)}) custom-call(f32[3,128,128]{2,1,0:T(8,128)S(1)} %get-tuple-element.6.final_vmem, f32[4,64]{1,0:T(4,128)S(1)} %get-tuple-element.7.tiles_vmem), custom_call_target="tpu_custom_call" | custom-call | tf_op jit(solution)/shard_map/pallas_call | solution.py:539

commit v2 on v1

--- a/solution.py
+++ b/solution.py
@@ -16,7 +16,6 @@
 ROWS = 128
 NODES = 125
 SHIFT = (100, -100, 20, -20, 4, -4)
-STRAIGHT_FROM = {1: 2, 0: 1, 2: 2}
 MESH = pl.DeviceIdType.MESH
 f32 = jnp.float32
 bf16 = jnp.bfloat16
@@ -27,9 +26,11 @@
     return (i == 0, i == 4, j == 0, j == 4, k == 0, k == 4)[face]
 
 
-TILE_FACES = [
-    [f for f in range(6) if any(on_face(f, n) for n in range(8 * t, min(8 * t + 8, NODES)))]
+FACE_TILES = [
+    (f, t)
     for t in range(ROWS // 8)
+    for f in range(6)
+    if any(on_face(f, n) for n in range(8 * t, min(8 * t + 8, NODES)))
 ]
 
 
@@ -59,7 +60,7 @@
     fwd_in, adj_in, stiff_hbm, proj_hbm, mat_hbm, nb_hbm, dest_hbm, count_hbm, smooth_hbm,
     fwd_out, tiles_out,
     stiff_in, proj_in, mat_in, nb_in, dest_in, count_in, smooth_in,
-    F, N, K, A, S, W, IDX, RIM, LIVE, send, rim, coef, coef_in, msg, mine, part, got, got2,
+    F, N, K, A, S, W, M, IDX, RIM, LIVE, send, rim, coef, coef_in, msg, mine, part, got, got2,
     in_s, small_s, rim_s, rim_r, coef_s, coef_r, a_s, a_r, b_s, b_r, rounds,
 ):
     me = lax.axis_index("mesh")
@@ -165,23 +166,25 @@
             device_id=(ev, lax.rem(me + 2, m_size)), device_id_type=MESH,
         )
 
-    def straight(f):
-        return STRAIGHT_FROM[f] if paired else 0
-
     def send_near(f):
         for c in range(3):
             rim_copy(f, 0, c).start()
 
     def send_far(f):
-        for c in range(straight(f), 3):
+        for c in range(3):
             rim_copy(f, 1, c).start()
+
+    def at_core(which, job):
+        @pl.when(core == which)
+        def _():
+            job()
 
     send_near(1)
     load_field(0)
     coef[...] = jnp.zeros((8, 128), f32)
     small[0].wait()
     coef[0:4, 0:4] = smooth_in[...]
-    send_far(1)
+    at_core(0, lambda: (send_far(1), send_near(0), send_far(0)))
     coef_copies = [
         remote(coef, coef_in.at[0], coef_s.at[0], coef_r.at[0], (ev, after)),
         remote(coef, coef_in.at[1], coef_s.at[1], coef_r.at[1], (ev, before)),
@@ -234,59 +237,52 @@
         both = mm(s_hi, hi) + (mm(s_hi, lo) + mm(s_lo, hi))
         return [both[:, 128 * c : 128 * (c + 1)] for c in range(3)]
 
-    def face_sums(read, relative_to):
+    def build_masks(which, relative_to):
+        here = [jnp.where(IDX[6 + f] == relative_to, 1.0, 0.0).astype(f32) for f in range(6)]
+        for n, (f, t) in enumerate(FACE_TILES):
+            M[which, n] = here[f] * W[f, 8 * t : 8 * t + 8, :]
+
+    def face_sums(read, which):
         sums = [None] * (ROWS // 8)
-        for f in range(6):
-            here = IDX[6 + f] == relative_to
-            for t in range(ROWS // 8):
-                if f in TILE_FACES[t]:
-                    g = jnp.where(here, read(f, 8 * t + SHIFT[f]), 0.0)
-                    g = g * W[f, 8 * t : 8 * t + 8, :]
-                    sums[t] = g if sums[t] is None else sums[t] + g
+        for n, (f, t) in enumerate(FACE_TILES):
+            g = read(f, 8 * t + SHIFT[f]) * M[which, n]
+            sums[t] = g if sums[t] is None else sums[t] + g
         return sums
 
     def own_pass(base):
-        def body(c, carry):
+        for c in range(3):
             sums = face_sums(lambda f, low: pick(F[base + c, low + PAD : low + 2 * PAD, :], IDX[f]), 0)
             for t in range(ROWS // 8):
                 at = pl.ds(8 * t, 8)
                 v = F[base + c, 8 * t + PAD : 8 * t + 2 * PAD, :]
                 acc = sums[t] - W[6, at, :] * v
                 N[base + c, at, :] = N[base + c, at, :] + (time_square * penalty) * acc
-            return carry
-
-        lax.fori_loop(0, 3, body, 0)
+
+    def arrive(f, k):
+        for c in range(3):
+            rim_copy(f, k, c).wait_recv()
+            if k == 0 and paired:
+
+                @pl.when(core == 1)
+                def _():
+                    relay_copy(f, c).start()
 
     def rim_pass(base, f, k, store, after_each=None):
         side = sides[k]
-        relative_to = jnp.where(side == 1, 1, m_size - 1)
-
-        def body(c, carry):
-            rim_copy(f, k, c).wait_recv()
-            if k == 0 and paired and straight(f) > 0:
-                if straight(f) == 3:
-                    relay_copy(f, c).start()
-                else:
-
-                    @pl.when(c < straight(f))
-                    def _():
-                        relay_copy(f, c).start()
-
+        for c in range(3):
             rim[f, side, c, 32:40, :] = pltpu.roll(rim[f, side, c, 0:8, :], 96, 1)
+        for c in range(3):
 
             def read(face, low):
                 at = low % 32
                 return pick(rim[f, side, c, at : at + 8, :], RIM[face, (low // 32) % 4])
 
-            sums = face_sums(read, relative_to)
+            sums = face_sums(read, 1 + k)
             for t in range(ROWS // 8):
                 old = N[base + c, 8 * t : 8 * t + 8, :]
                 store(c, t, old + (time_square * penalty) * sums[t])
             if after_each is not None:
                 after_each(c)
-            return carry
-
-        lax.fori_loop(0, 3, body, 0)
 
     def send_next(c):
         send[2, c] = pack(c)
@@ -298,6 +294,7 @@
 
         return store
 
+    build_masks(0, 0)
     st_f = strain(0)
     st_a = strain(3)
     energy = jnp.zeros((ROWS, 128), f32)
@@ -307,11 +304,15 @@
         N[c] = vf - time_square * material * st_f[c]
         N[3 + c] = F[3 + c, PAD : PAD + ROWS, :] - time_square * material * st_a[c]
     K[...] = energy
-    send_near(0)
+    if not paired:
+        at_core(1, lambda: (send_far(1), send_near(0), send_far(0)))
+    else:
+        at_core(1, lambda: send_near(0))
     own_pass(3)
-    send_far(0)
     own_pass(0)
     next_round(0)
+    for k in range(2):
+        build_masks(1 + k, jnp.where(sides[k] == 1, 1, m_size - 1))
 
     def keep_adjoint(c, t, value):
         F[3 + c, 8 * t + PAD : 8 * t + 2 * PAD, :] = LIVE[...] * value
@@ -324,14 +325,23 @@
         F[c, at, :] = value
         K[line, :] = K[line, :] + value * A[c, line, :]
 
+    arrive(1, 0)
     rim_pass(3, 1, 0, add(3))
     next_round(1)
-    rim_pass(0, 0, 0, add(0))
+    if paired:
+        at_core(1, lambda: arrive(0, 0))
+    arrive(1, 1)
     rim_pass(3, 1, 1, keep_adjoint)
     for n in range(2, n_rounds):
         next_round(n)
     for c, value in enumerate(strain(3)):
         A[c] = value
+    if paired:
+        at_core(0, lambda: arrive(0, 0))
+    else:
+        arrive(0, 0)
+    rim_pass(0, 0, 0, add(0))
+    arrive(0, 1)
     rim_pass(0, 0, 1, keep_forward, send_next)
 
     elements = F.shape[-1]
@@ -370,7 +380,10 @@
             for o in range(1, m_size)
         ]
 
-    send_far(2)
+    if paired:
+        at_core(0, lambda: send_far(2))
+    else:
+        send_far(2)
 
     st_f = strain(0)
     for c in range(3):
@@ -401,7 +414,9 @@
     def final(c, t, value):
         fwd_out[c, 8 * t : 8 * t + 8, :] = LIVE[...] * value
 
+    arrive(2, 0)
     rim_pass(0, 2, 0, add(0))
+    arrive(2, 1)
     rim_pass(0, 2, 1, final)
 
     for copy in coef_copies[2:]:
@@ -518,6 +533,7 @@
                 pltpu.VMEM((3, ROWS, 128), f32),
                 pltpu.VMEM((ROWS, ROWS), f32),
                 pltpu.VMEM((7, ROWS, 128), f32),
+                pltpu.VMEM((3, len(FACE_TILES), 8, 128), f32),
                 pltpu.VMEM((12, 8, 128), jnp.int32),
                 pltpu.VMEM((6, 4, 8, 128), jnp.int32),
                 pltpu.VMEM((8, 128), f32),

time: 21 us -> 19.9 us (0.948)
  Pallas kernels: 19.6 us -> 18.4 us
    pallas_call x1, Pallas kernels: 18.9 us -> 17.7 us  [per_device(): pl.pallas_call(functools.partial(kernel, m_size, e_size), out_shape=(pltp...]
where the time goes in v2:
time: 19.9 us; the launch traced here: 19.7 us
  Pallas kernels  18.4 us (92%)
  between operations  1.29 us (6%)
    pallas_call x1, Pallas kernels, per_device(): pl.pallas_call(functools.partial(kernel, m_size, e_size), out_shape=(pltp...  17.7 us
    pallas_call x1, Pallas kernels, per_device(): pl.pallas_call(write_out, out_shape=(pltpu.HBM(line, f32), pltpu.HBM((wid...  0.71 us

profile of v2, /device:TPU:0, one launch (start us, length us, event | category | flops | bytes accessed | tf_op | source)
XLA Modules:
  0.0 19.7 jit_solution(13934082066281796485)
XLA Ops:
  1.3 17.7 %shard_map.104 = (f32[3,128,128]{2,1,0:T(8,128)S(1)}, f32[4,64]{1,0:T(4,128)S(1)}) custom-call(f32[375,1,128]{2,1,0:T(1,128)} %bitcast.6, f32[375,1,128]{2,1,0:T(1,128)} %bitcast.7, f32[125,125]{1,0:T(8,128)} %stiff_hbm.1, f32[64,125]{1,0:T(8,128)} %bitcast.8, f32[1,128]{1,0:T(1,128)} %mat_hbm.1, s32[6,1,128]{2,1,0:T(1,128)} %bitcast.9, s32[1,128]{1,0:T(1,128)} %dest_hbm.1, ...), custom_call_target="tpu_custom_call" | custom-call | tf_op jit(solution)/shard_map/pallas_call | solution.py:520
  19.0 0.7 %shard_map.105 = (f32[375,1,128]{2,1,0:T(1,128)}, f32[4,64]{1,0:T(4,128)}) custom-call(f32[3,128,128]{2,1,0:T(8,128)S(1)} %get-tuple-element.6.final_vmem, f32[4,64]{1,0:T(4,128)S(1)} %get-tuple-element.7.tiles_vmem), custom_call_target="tpu_custom_call" | custom-call | tf_op jit(solution)/shard_map/pallas_call | solution.py:555

commit v3 on v2

--- a/solution.py
+++ b/solution.py
@@ -28,8 +28,8 @@
 
 FACE_TILES = [
     (f, t)
+    for f in range(6)
     for t in range(ROWS // 8)
-    for f in range(6)
     if any(on_face(f, n) for n in range(8 * t, min(8 * t + 8, NODES)))
 ]
 
@@ -44,7 +44,11 @@
 
 
 def pick(x, index):
-    return jnp.take_along_axis(x, index, axis=1, mode="promise_in_bounds")
+    dims = lax.GatherDimensionNumbers(
+        offset_dims=(), collapsed_slice_dims=(1,), start_index_map=(1,),
+        operand_batching_dims=(0,), start_indices_batching_dims=(0,),
+    )
+    return lax.gather(x, index[:, :, None], dims, (1, 1), mode=lax.GatherScatterMode.PROMISE_IN_BOUNDS)
 
 
 def is_direct(m_size, e_size):
@@ -60,7 +64,7 @@
     fwd_in, adj_in, stiff_hbm, proj_hbm, mat_hbm, nb_hbm, dest_hbm, count_hbm, smooth_hbm,
     fwd_out, tiles_out,
     stiff_in, proj_in, mat_in, nb_in, dest_in, count_in, smooth_in,
-    F, N, K, A, S, W, M, IDX, RIM, LIVE, send, rim, coef, coef_in, msg, mine, part, got, got2,
+    F, N, K, A, S, W, M, IDX, RIM, LIVE, send, rim, U, coef, coef_in, msg, mine, part, got, got2,
     in_s, small_s, rim_s, rim_r, coef_s, coef_r, a_s, a_r, b_s, b_r, rounds,
 ):
     me = lax.axis_index("mesh")
@@ -149,19 +153,18 @@
     first = 1 - lax.rem(me, 2) if paired else 0
     second = 1 - first
     sides = (first, second)
-    low32 = pl.ds(0, 32)
 
     def rim_copy(f, k, c):
         slot = sides[1 - k] if paired else sides[k]
         return pltpu.make_async_remote_copy(
-            src_ref=send.at[f, c], dst_ref=rim.at[f, slot, c, low32],
+            src_ref=send.at[f, c], dst_ref=rim.at[f, slot, c],
             send_sem=rim_s.at[f, k, c], recv_sem=rim_r.at[f, k, c],
             device_id=(ev, jnp.where(slot == 0, after, before)), device_id_type=MESH,
         )
 
     def relay_copy(f, c):
         return pltpu.make_async_remote_copy(
-            src_ref=rim.at[f, first, c, low32], dst_ref=rim.at[f, second, c, low32],
+            src_ref=rim.at[f, first, c], dst_ref=rim.at[f, second, c],
             send_sem=rim_s.at[f, 1, c], recv_sem=rim_r.at[f, 1, c],
             device_id=(ev, lax.rem(me + 2, m_size)), device_id_type=MESH,
         )
@@ -224,8 +227,11 @@
     for f in range(6):
         IDX[f] = jnp.broadcast_to(slot[f : f + 1], (8, 128))
         IDX[6 + f] = jnp.broadcast_to(relative[f : f + 1], (8, 128))
-        for g in range(4):
-            RIM[f, g] = jnp.broadcast_to((slot[f : f + 1] & 31) + 32 * g, (8, 128))
+        far = jnp.where(relative[f : f + 1] == jnp.where(second == 1, 1, m_size - 1), 32, 0)
+        RIM[f] = jnp.broadcast_to((slot[f : f + 1] & 31) + far, (8, 128))
+    for c in range(3):
+        U[c, 0:PAD, :] = zero8
+        U[c, PAD + ROWS : ROWS + 2 * PAD, :] = zero8
     S[...] = jnp.zeros((ROWS, ROWS), f32)
     S[0:NODES, 0:NODES] = stiff_in[...]
     s_hi, s_lo = split(S[...])
@@ -237,10 +243,9 @@
         both = mm(s_hi, hi) + (mm(s_hi, lo) + mm(s_lo, hi))
         return [both[:, 128 * c : 128 * (c + 1)] for c in range(3)]
 
-    def build_masks(which, relative_to):
-        here = [jnp.where(IDX[6 + f] == relative_to, 1.0, 0.0).astype(f32) for f in range(6)]
+    def build_masks(which, here):
         for n, (f, t) in enumerate(FACE_TILES):
-            M[which, n] = here[f] * W[f, 8 * t : 8 * t + 8, :]
+            M[which, n] = jnp.where(here(IDX[6 + f]), W[f, 8 * t : 8 * t + 8, :], 0.0)
 
     def face_sums(read, which):
         sums = [None] * (ROWS // 8)
@@ -267,34 +272,29 @@
                 def _():
                     relay_copy(f, c).start()
 
-    def rim_pass(base, f, k, store, after_each=None):
+    def unpack(f, k):
         side = sides[k]
         for c in range(3):
-            rim[f, side, c, 32:40, :] = pltpu.roll(rim[f, side, c, 0:8, :], 96, 1)
-        for c in range(3):
-
-            def read(face, low):
-                at = low % 32
-                return pick(rim[f, side, c, at : at + 8, :], RIM[face, (low // 32) % 4])
-
-            sums = face_sums(read, 1 + k)
+            for g in range(4):
+                at = pl.ds(PAD + 32 * g, 32)
+                turn = (32 * k - 32 * g) % 128
+                part = rim[f, side, c]
+                part = pltpu.roll(part, turn, 1) if turn else part
+                U[c, at, :] = part if k == 0 else jnp.where(lane < 32, U[c, at, :], part)
+
+    def rim_pass(base, store, after_each=None):
+        for c in range(3):
+            sums = face_sums(lambda face, low: pick(U[c, low + PAD : low + 2 * PAD, :], RIM[face]), 1)
             for t in range(ROWS // 8):
                 old = N[base + c, 8 * t : 8 * t + 8, :]
                 store(c, t, old + (time_square * penalty) * sums[t])
             if after_each is not None:
                 after_each(c)
 
-    def send_next(c):
+    def pack_next(c):
         send[2, c] = pack(c)
-        rim_copy(2, 0, c).start()
-
-    def add(base):
-        def store(c, t, value):
-            N[base + c, 8 * t : 8 * t + 8, :] = value
-
-        return store
-
-    build_masks(0, 0)
+
+    build_masks(0, lambda relative: relative == 0)
     st_f = strain(0)
     st_a = strain(3)
     energy = jnp.zeros((ROWS, 128), f32)
@@ -311,8 +311,7 @@
     own_pass(3)
     own_pass(0)
     next_round(0)
-    for k in range(2):
-        build_masks(1 + k, jnp.where(sides[k] == 1, 1, m_size - 1))
+    build_masks(1, lambda relative: (relative == 1) | (relative == m_size - 1))
 
     def keep_adjoint(c, t, value):
         F[3 + c, 8 * t + PAD : 8 * t + 2 * PAD, :] = LIVE[...] * value
@@ -326,12 +325,13 @@
         K[line, :] = K[line, :] + value * A[c, line, :]
 
     arrive(1, 0)
-    rim_pass(3, 1, 0, add(3))
+    unpack(1, 0)
     next_round(1)
     if paired:
         at_core(1, lambda: arrive(0, 0))
     arrive(1, 1)
-    rim_pass(3, 1, 1, keep_adjoint)
+    unpack(1, 1)
+    rim_pass(3, keep_adjoint)
     for n in range(2, n_rounds):
         next_round(n)
     for c, value in enumerate(strain(3)):
@@ -340,9 +340,10 @@
         at_core(0, lambda: arrive(0, 0))
     else:
         arrive(0, 0)
-    rim_pass(0, 0, 0, add(0))
+    unpack(0, 0)
     arrive(0, 1)
-    rim_pass(0, 0, 1, keep_forward, send_next)
+    unpack(0, 1)
+    rim_pass(0, keep_forward, pack_next)
 
     elements = F.shape[-1]
     width = smooth_in.shape[1]
@@ -380,6 +381,7 @@
             for o in range(1, m_size)
         ]
 
+    send_near(2)
     if paired:
         at_core(0, lambda: send_far(2))
     else:
@@ -415,9 +417,10 @@
         fwd_out[c, 8 * t : 8 * t + 8, :] = LIVE[...] * value
 
     arrive(2, 0)
-    rim_pass(0, 2, 0, add(0))
+    unpack(2, 0)
     arrive(2, 1)
-    rim_pass(0, 2, 1, final)
+    unpack(2, 1)
+    rim_pass(0, final)
 
     for copy in coef_copies[2:]:
         copy.wait_recv()
@@ -533,12 +536,13 @@
                 pltpu.VMEM((3, ROWS, 128), f32),
                 pltpu.VMEM((ROWS, ROWS), f32),
                 pltpu.VMEM((7, ROWS, 128), f32),
-                pltpu.VMEM((3, len(FACE_TILES), 8, 128), f32),
+                pltpu.VMEM((2, len(FACE_TILES), 8, 128), f32),
                 pltpu.VMEM((12, 8, 128), jnp.int32),
-                pltpu.VMEM((6, 4, 8, 128), jnp.int32),
+                pltpu.VMEM((6, 8, 128), jnp.int32),
                 pltpu.VMEM((8, 128), f32),
                 pltpu.VMEM((3, 3, 32, 128), f32),
-                pltpu.VMEM((3, 2, 3, 40, 128), f32),
+                pltpu.VMEM((3, 2, 3, 32, 128), f32),
+                pltpu.VMEM((3, 144, 128), f32),
                 pltpu.VMEM((8, 128), f32),
                 pltpu.VMEM((4, 8, 128), f32),
                 pltpu.VMEM((m_size, e_size, width, 128), f32),

time: 19.9 us -> 19.3 us (0.970)
  Pallas kernels: 18.4 us -> 17.9 us
    pallas_call x1, Pallas kernels: 17.7 us -> 17.2 us  [per_device(): pl.pallas_call(functools.partial(kernel, m_size, e_size), out_shape=(pltp...]
where the time goes in v3:
time: 19.3 us; the launch traced here: 19.2 us
  Pallas kernels  17.9 us (93%)
  between operations  1.29 us (7%)
    pallas_call x1, Pallas kernels, per_device(): pl.pallas_call(functools.partial(kernel, m_size, e_size), out_shape=(pltp...  17.2 us
    pallas_call x1, Pallas kernels, per_device(): pl.pallas_call(write_out, out_shape=(pltpu.HBM(line, f32), pltpu.HBM((wid...  0.71 us

profile of v3, /device:TPU:0, one launch (start us, length us, event | category | flops | bytes accessed | tf_op | source)
XLA Modules:
  0.0 19.2 jit_solution(6053141411907325908)
XLA Ops:
  1.3 17.2 %shard_map.104 = (f32[3,128,128]{2,1,0:T(8,128)S(1)}, f32[4,64]{1,0:T(4,128)S(1)}) custom-call(f32[375,1,128]{2,1,0:T(1,128)} %bitcast.6, f32[375,1,128]{2,1,0:T(1,128)} %bitcast.7, f32[125,125]{1,0:T(8,128)} %stiff_hbm.1, f32[64,125]{1,0:T(8,128)} %bitcast.8, f32[1,128]{1,0:T(1,128)} %mat_hbm.1, s32[6,1,128]{2,1,0:T(1,128)} %bitcast.9, s32[1,128]{1,0:T(1,128)} %dest_hbm.1, ...), custom_call_target="tpu_custom_call" | custom-call | tf_op jit(solution)/shard_map/pallas_call | solution.py:523
  18.5 0.7 %shard_map.105 = (f32[375,1,128]{2,1,0:T(1,128)}, f32[4,64]{1,0:T(4,128)}) custom-call(f32[3,128,128]{2,1,0:T(8,128)S(1)} %get-tuple-element.6.final_vmem, f32[4,64]{1,0:T(4,128)S(1)} %get-tuple-element.7.tiles_vmem), custom_call_target="tpu_custom_call" | custom-call | tf_op jit(solution)/shard_map/pallas_call | solution.py:559

commit v4 on v3

--- a/solution.py
+++ b/solution.py
@@ -26,6 +26,9 @@
     return (i == 0, i == 4, j == 0, j == 4, k == 0, k == 4)[face]
 
 
+RIM_NODES = [n for n in range(NODES) if any(on_face(f, n) for f in range(6))]
+RIM_PLACE = {n: at for at, n in enumerate(RIM_NODES)}
+RIM_ROWS = -(-len(RIM_NODES) // 4)
 FACE_TILES = [
     (f, t)
     for f in range(6)
@@ -49,6 +52,22 @@
         operand_batching_dims=(0,), start_indices_batching_dims=(0,),
     )
     return lax.gather(x, index[:, :, None], dims, (1, 1), mode=lax.GatherScatterMode.PROMISE_IN_BOUNDS)
+
+
+def gather_rows(load, places):
+    pieces = {}
+    for r, place in enumerate(places):
+        if place is not None:
+            pieces.setdefault(place - r, []).append(r)
+    sublane = lax.broadcasted_iota(jnp.int32, (8, 128), 0)
+    value = None
+    for shift, members in pieces.items():
+        piece = load(shift)
+        if value is None:
+            value = piece
+        else:
+            value = jnp.where((sublane >= members[0]) & (sublane <= members[-1]), piece, value)
+    return load(0) if value is None else value
 
 
 def is_direct(m_size, e_size):
@@ -125,22 +144,26 @@
         F[fc, 0:PAD, :] = zero8
         F[fc, PAD + NODES : 144, :] = jnp.zeros((144 - PAD - NODES, 128), f32)
 
-    def pack(fc):
-        wide = [F[fc, PAD + 32 * g : PAD + 32 * g + 32, :] for g in range(4)]
-        turned = [wide[0]] + [pltpu.roll(wide[g], 32 * g, 1) for g in range(1, 4)]
-        return jnp.where(
-            lane < 64, jnp.where(lane < 32, turned[0], turned[1]),
-            jnp.where(lane < 96, turned[2], turned[3]),
-        )
-
-    def load_field(f):
+    def pack(f, c, fc):
+        for v in range(-(-RIM_ROWS // 8)):
+            parts = []
+            for g in range(4):
+                inside = range(RIM_ROWS * g + 8 * v, min(RIM_ROWS * (g + 1), RIM_ROWS * g + 8 * v + 8))
+                places = [RIM_NODES[n] if n < len(RIM_NODES) else None for n in inside]
+                part = gather_rows(lambda low: F[fc, low + PAD : low + 2 * PAD, :], places)
+                parts.append(pltpu.roll(part, 32 * g, 1) if g else part)
+            send[f, c, 8 * v : 8 * v + 8, :] = jnp.where(
+                lane < 64, jnp.where(lane < 32, parts[0], parts[1]),
+                jnp.where(lane < 96, parts[2], parts[3]),
+            )
+
+    def load_field(f, then=None):
         for c in range(3):
             loads[3 * f + c].wait()
-            send[f, c] = pack(3 * f + c)
-
-    load_field(1)
-
-    pl.semaphore_wait(barrier, near_count + (m_size - 1))
+            pack(f, c, 3 * f + c)
+            if then is not None:
+                then(c)
+
 
     def remote(src, dst, s, r, device):
         copy = pltpu.make_async_remote_copy(
@@ -153,18 +176,19 @@
     first = 1 - lax.rem(me, 2) if paired else 0
     second = 1 - first
     sides = (first, second)
+    used = pl.ds(0, RIM_ROWS)
 
     def rim_copy(f, k, c):
         slot = sides[1 - k] if paired else sides[k]
         return pltpu.make_async_remote_copy(
-            src_ref=send.at[f, c], dst_ref=rim.at[f, slot, c],
+            src_ref=send.at[f, c, used], dst_ref=rim.at[f, slot, c, used],
             send_sem=rim_s.at[f, k, c], recv_sem=rim_r.at[f, k, c],
             device_id=(ev, jnp.where(slot == 0, after, before)), device_id_type=MESH,
         )
 
     def relay_copy(f, c):
         return pltpu.make_async_remote_copy(
-            src_ref=rim.at[f, first, c], dst_ref=rim.at[f, second, c],
+            src_ref=rim.at[f, first, c, used], dst_ref=rim.at[f, second, c, used],
             send_sem=rim_s.at[f, 1, c], recv_sem=rim_r.at[f, 1, c],
             device_id=(ev, lax.rem(me + 2, m_size)), device_id_type=MESH,
         )
@@ -182,7 +206,12 @@
         def _():
             job()
 
-    send_near(1)
+    def near_of(c):
+        if c == 0:
+            pl.semaphore_wait(barrier, near_count + (m_size - 1))
+        rim_copy(1, 0, c).start()
+
+    load_field(1, near_of)
     load_field(0)
     coef[...] = jnp.zeros((8, 128), f32)
     small[0].wait()
@@ -231,7 +260,7 @@
         RIM[f] = jnp.broadcast_to((slot[f : f + 1] & 31) + far, (8, 128))
     for c in range(3):
         U[c, 0:PAD, :] = zero8
-        U[c, PAD + ROWS : ROWS + 2 * PAD, :] = zero8
+        U[c, PAD + 4 * RIM_ROWS :, :] = jnp.zeros((U.shape[1] - PAD - 4 * RIM_ROWS, 128), f32)
     S[...] = jnp.zeros((ROWS, ROWS), f32)
     S[0:NODES, 0:NODES] = stiff_in[...]
     s_hi, s_lo = split(S[...])
@@ -250,13 +279,17 @@
     def face_sums(read, which):
         sums = [None] * (ROWS // 8)
         for n, (f, t) in enumerate(FACE_TILES):
-            g = read(f, 8 * t + SHIFT[f]) * M[which, n]
+            g = read(f, t) * M[which, n]
             sums[t] = g if sums[t] is None else sums[t] + g
         return sums
 
     def own_pass(base):
         for c in range(3):
-            sums = face_sums(lambda f, low: pick(F[base + c, low + PAD : low + 2 * PAD, :], IDX[f]), 0)
+            def read(f, t):
+                at = 8 * t + SHIFT[f] + PAD
+                return pick(F[base + c, at : at + 8, :], IDX[f])
+
+            sums = face_sums(read, 0)
             for t in range(ROWS // 8):
                 at = pl.ds(8 * t, 8)
                 v = F[base + c, 8 * t + PAD : 8 * t + 2 * PAD, :]
@@ -276,23 +309,27 @@
         side = sides[k]
         for c in range(3):
             for g in range(4):
-                at = pl.ds(PAD + 32 * g, 32)
+                at = pl.ds(PAD + RIM_ROWS * g, RIM_ROWS)
                 turn = (32 * k - 32 * g) % 128
-                part = rim[f, side, c]
+                part = rim[f, side, c, 0:RIM_ROWS, :]
                 part = pltpu.roll(part, turn, 1) if turn else part
                 U[c, at, :] = part if k == 0 else jnp.where(lane < 32, U[c, at, :], part)
 
-    def rim_pass(base, store, after_each=None):
+    def rim_pass(base, store):
         for c in range(3):
-            sums = face_sums(lambda face, low: pick(U[c, low + PAD : low + 2 * PAD, :], RIM[face]), 1)
+
+            def read(f, t):
+                places = [
+                    RIM_PLACE[8 * t + r + SHIFT[f]] if 8 * t + r < NODES and on_face(f, 8 * t + r) else None
+                    for r in range(8)
+                ]
+                rows = gather_rows(lambda low: U[c, low + PAD : low + 2 * PAD, :], places)
+                return pick(rows, RIM[f])
+
+            sums = face_sums(read, 1)
             for t in range(ROWS // 8):
                 old = N[base + c, 8 * t : 8 * t + 8, :]
                 store(c, t, old + (time_square * penalty) * sums[t])
-            if after_each is not None:
-                after_each(c)
-
-    def pack_next(c):
-        send[2, c] = pack(c)
 
     build_masks(0, lambda relative: relative == 0)
     st_f = strain(0)
@@ -343,7 +380,7 @@
     unpack(0, 0)
     arrive(0, 1)
     unpack(0, 1)
-    rim_pass(0, keep_forward, pack_next)
+    rim_pass(0, keep_forward)
 
     elements = F.shape[-1]
     width = smooth_in.shape[1]
@@ -381,6 +418,8 @@
             for o in range(1, m_size)
         ]
 
+    for c in range(3):
+        pack(2, c, c)
     send_near(2)
     if paired:
         at_core(0, lambda: send_far(2))
@@ -542,7 +581,7 @@
                 pltpu.VMEM((8, 128), f32),
                 pltpu.VMEM((3, 3, 32, 128), f32),
                 pltpu.VMEM((3, 2, 3, 32, 128), f32),
-                pltpu.VMEM((3, 144, 128), f32),
+                pltpu.VMEM((3, 120, 128), f32),
                 pltpu.VMEM((8, 128), f32),
                 pltpu.VMEM((4, 8, 128), f32),
                 pltpu.VMEM((m_size, e_size, width, 128), f32),

time: 19.3 us -> 19 us (0.984)
  Pallas kernels: 17.9 us -> 17.5 us
    pallas_call x1, Pallas kernels: 17.2 us -> 16.8 us  [per_device(): pl.pallas_call(functools.partial(kernel, m_size, e_size), out_shape=(pltp...]
where the time goes in v4:
time: 19 us; the launch traced here: 18.8 us
  Pallas kernels  17.5 us (92%)
  between operations  1.29 us (7%)
    pallas_call x1, Pallas kernels, per_device(): pl.pallas_call(functools.partial(kernel, m_size, e_size), out_shape=(pltp...  16.8 us
    pallas_call x1, Pallas kernels, per_device(): pl.pallas_call(write_out, out_shape=(pltpu.HBM(line, f32), pltpu.HBM((wid...  0.71 us

profile of v4, /device:TPU:0, one launch (start us, length us, event | category | flops | bytes accessed | tf_op | source)
XLA Modules:
  0.0 18.8 jit_solution(13429505475741818348)
XLA Ops:
  1.3 16.8 %shard_map.104 = (f32[3,128,128]{2,1,0:T(8,128)S(1)}, f32[4,64]{1,0:T(4,128)S(1)}) custom-call(f32[375,1,128]{2,1,0:T(1,128)} %bitcast.6, f32[375,1,128]{2,1,0:T(1,128)} %bitcast.7, f32[125,125]{1,0:T(8,128)} %stiff_hbm.1, f32[64,125]{1,0:T(8,128)} %bitcast.8, f32[1,128]{1,0:T(1,128)} %mat_hbm.1, s32[6,1,128]{2,1,0:T(1,128)} %bitcast.9, s32[1,128]{1,0:T(1,128)} %dest_hbm.1, ...), custom_call_target="tpu_custom_call" | custom-call | tf_op jit(solution)/shard_map/pallas_call | solution.py:562
  18.1 0.7 %shard_map.105 = (f32[375,1,128]{2,1,0:T(1,128)}, f32[4,64]{1,0:T(4,128)}) custom-call(f32[3,128,128]{2,1,0:T(8,128)S(1)} %get-tuple-element.6.final_vmem, f32[4,64]{1,0:T(4,128)S(1)} %get-tuple-element.7.tiles_vmem), custom_call_target="tpu_custom_call" | custom-call | tf_op jit(solution)/shard_map/pallas_call | solution.py:598

commit v5 on v4

--- a/solution.py
+++ b/solution.py
@@ -16,6 +16,7 @@
 ROWS = 128
 NODES = 125
 SHIFT = (100, -100, 20, -20, 4, -4)
+RELAYED = (0,)
 MESH = pl.DeviceIdType.MESH
 f32 = jnp.float32
 bf16 = jnp.bfloat16
@@ -206,17 +207,18 @@
         def _():
             job()
 
-    def near_of(c):
+    def far_of(c):
         if c == 0:
             pl.semaphore_wait(barrier, near_count + (m_size - 1))
-        rim_copy(1, 0, c).start()
-
-    load_field(1, near_of)
+        rim_copy(1, 1, c).start()
+
+    load_field(1, far_of)
+    send_near(1)
     load_field(0)
     coef[...] = jnp.zeros((8, 128), f32)
     small[0].wait()
     coef[0:4, 0:4] = smooth_in[...]
-    at_core(0, lambda: (send_far(1), send_near(0), send_far(0)))
+    at_core(0, lambda: (send_far(0), send_near(0)))
     coef_copies = [
         remote(coef, coef_in.at[0], coef_s.at[0], coef_r.at[0], (ev, after)),
         remote(coef, coef_in.at[1], coef_s.at[1], coef_r.at[1], (ev, before)),
@@ -299,7 +301,7 @@
     def arrive(f, k):
         for c in range(3):
             rim_copy(f, k, c).wait_recv()
-            if k == 0 and paired:
+            if k == 0 and paired and f in RELAYED:
 
                 @pl.when(core == 1)
                 def _():
@@ -331,6 +333,8 @@
                 old = N[base + c, 8 * t : 8 * t + 8, :]
                 store(c, t, old + (time_square * penalty) * sums[t])
 
+    if paired:
+        at_core(1, lambda: send_near(0))
     build_masks(0, lambda relative: relative == 0)
     st_f = strain(0)
     st_a = strain(3)
@@ -342,9 +346,9 @@
         N[3 + c] = F[3 + c, PAD : PAD + ROWS, :] - time_square * material * st_a[c]
     K[...] = energy
     if not paired:
-        at_core(1, lambda: (send_far(1), send_near(0), send_far(0)))
+        at_core(1, lambda: (send_near(0), send_far(0)))
     else:
-        at_core(1, lambda: send_near(0))
+        pass
     own_pass(3)
     own_pass(0)
     next_round(0)
@@ -364,7 +368,7 @@
     arrive(1, 0)
     unpack(1, 0)
     next_round(1)
-    if paired:
+    if paired and 0 in RELAYED:
         at_core(1, lambda: arrive(0, 0))
     arrive(1, 1)
     unpack(1, 1)
@@ -373,7 +377,7 @@
         next_round(n)
     for c, value in enumerate(strain(3)):
         A[c] = value
-    if paired:
+    if paired and 0 in RELAYED:
         at_core(0, lambda: arrive(0, 0))
     else:
         arrive(0, 0)
@@ -382,6 +386,17 @@
     unpack(0, 1)
     rim_pass(0, keep_forward)
 
+    def send_second():
+        for c in range(3):
+            pack(2, c, c)
+        if paired and 2 in RELAYED:
+            at_core(0, lambda: send_far(2))
+        else:
+            send_far(2)
+        send_near(2)
+
+    ahead = chip < chips // 2
+    pl.when(ahead)(send_second)
     elements = F.shape[-1]
     width = smooth_in.shape[1]
     scale = math.sqrt(width / elements) / STEPS
@@ -418,13 +433,7 @@
             for o in range(1, m_size)
         ]
 
-    for c in range(3):
-        pack(2, c, c)
-    send_near(2)
-    if paired:
-        at_core(0, lambda: send_far(2))
-    else:
-        send_far(2)
+    pl.when(jnp.logical_not(ahead))(send_second)
 
     st_f = strain(0)
     for c in range(3):

time: 19 us -> 18.7 us (0.984)
  Pallas kernels: 17.5 us -> 17.2 us
    pallas_call x1, Pallas kernels: 16.8 us -> 16.5 us  [per_device(): pl.pallas_call(functools.partial(kernel, m_size, e_size), out_shape=(pltp...]
where the time goes in v5:
time: 18.7 us; the launch traced here: 18.5 us
  Pallas kernels  17.2 us (92%)
  between operations  1.29 us (7%)
    pallas_call x1, Pallas kernels, per_device(): pl.pallas_call(functools.partial(kernel, m_size, e_size), out_shape=(pltp...  16.5 us
    pallas_call x1, Pallas kernels, per_device(): pl.pallas_call(write_out, out_shape=(pltpu.HBM(line, f32), pltpu.HBM((wid...  0.71 us

profile of v5, /device:TPU:0, one launch (start us, length us, event | category | flops | bytes accessed | tf_op | source)
XLA Modules:
  0.0 18.5 jit_solution(596284033947169977)
XLA Ops:
  1.3 16.5 %shard_map.104 = (f32[3,128,128]{2,1,0:T(8,128)S(1)}, f32[4,64]{1,0:T(4,128)S(1)}) custom-call(f32[375,1,128]{2,1,0:T(1,128)} %bitcast.6, f32[375,1,128]{2,1,0:T(1,128)} %bitcast.7, f32[125,125]{1,0:T(8,128)} %stiff_hbm.1, f32[64,125]{1,0:T(8,128)} %bitcast.8, f32[1,128]{1,0:T(1,128)} %mat_hbm.1, s32[6,1,128]{2,1,0:T(1,128)} %bitcast.9, s32[1,128]{1,0:T(1,128)} %dest_hbm.1, ...), custom_call_target="tpu_custom_call" | custom-call | tf_op jit(solution)/shard_map/pallas_call | solution.py:571
  17.8 0.7 %shard_map.105 = (f32[375,1,128]{2,1,0:T(1,128)}, f32[4,64]{1,0:T(4,128)}) custom-call(f32[3,128,128]{2,1,0:T(8,128)S(1)} %get-tuple-element.6.final_vmem, f32[4,64]{1,0:T(4,128)S(1)} %get-tuple-element.7.tiles_vmem), custom_call_target="tpu_custom_call" | custom-call | tf_op jit(solution)/shard_map/pallas_call | solution.py:607

commit v6 on v5

--- a/solution.py
+++ b/solution.py
@@ -73,10 +73,6 @@
 
 def is_direct(m_size, e_size):
     return m_size * e_size <= 64
-
-
-def round_count(m_size, e_size):
-    return max(e_size // 2 - 1, 1) if is_direct(m_size, e_size) else max(e_size // 2 - 2, 0)
 
 
 def kernel(
@@ -105,8 +101,8 @@
         near += [((2 * (chip + step) + c, me), inside) for c in range(2)]
     near_count = 1 + 2 * ((chip > 0).astype(jnp.int32) + (chip < chips - 1).astype(jnp.int32))
 
-    def greet(sem):
-        for device, inside in near:
+    def greet(sem, devices):
+        for device, inside in devices:
             if inside is None:
                 pl.semaphore_signal(sem, inc=1, device_id=device, device_id_type=MESH)
             else:
@@ -119,7 +115,7 @@
         pl.semaphore_signal(
             barrier, inc=1, device_id=(ev, lax.rem(me + o, m_size)), device_id_type=MESH
         )
-    greet(barrier)
+    greet(barrier, near)
 
     loads = {}
     for fc in (3, 4, 5, 0, 1, 2):
@@ -216,6 +212,15 @@
     send_near(1)
     load_field(0)
     coef[...] = jnp.zeros((8, 128), f32)
+
+    @pl.when(ev == 0)
+    def _():
+        coef_in[2] = jnp.zeros((8, 128), f32)
+
+    @pl.when(ev == e_size - 1)
+    def _():
+        coef_in[3] = jnp.zeros((8, 128), f32)
+
     small[0].wait()
     coef[0:4, 0:4] = smooth_in[...]
     at_core(0, lambda: (send_far(0), send_near(0)))
@@ -223,15 +228,22 @@
         remote(coef, coef_in.at[0], coef_s.at[0], coef_r.at[0], (ev, after)),
         remote(coef, coef_in.at[1], coef_s.at[1], coef_r.at[1], (ev, before)),
     ]
-    n_rounds = round_count(m_size, e_size)
-    if n_rounds:
-        greet(rounds.at[0])
-
-    def next_round(n):
-        if n < n_rounds:
-            pl.semaphore_wait(rounds.at[n], near_count)
-            if n + 1 < n_rounds:
-                greet(rounds.at[n + 1])
+    beside, above, below = near[:1], near[1:3], near[3:]
+    is_first, is_last = chip == 0, chip == chips - 1
+
+    def wait_up():
+        pl.semaphore_wait(rounds.at[0], 2)
+        greet(rounds.at[0], above)
+
+    def wait_down():
+        pl.semaphore_wait(rounds.at[1], 2)
+        greet(rounds.at[1], below)
+
+    greet(rounds.at[2], beside)
+    pl.when(is_first)(lambda: greet(rounds.at[0], above))
+    pl.when(is_last)(lambda: greet(rounds.at[1], below))
+    between = jnp.logical_not(is_first | is_last)
+    turns = between & (chip == chips - 2)
 
     for load in small[1:]:
         load.wait()
@@ -351,7 +363,7 @@
         pass
     own_pass(3)
     own_pass(0)
-    next_round(0)
+    pl.when(between)(wait_up)
     build_masks(1, lambda relative: (relative == 1) | (relative == m_size - 1))
 
     def keep_adjoint(c, t, value):
@@ -367,14 +379,13 @@
 
     arrive(1, 0)
     unpack(1, 0)
-    next_round(1)
+    pl.when(turns)(wait_down)
     if paired and 0 in RELAYED:
         at_core(1, lambda: arrive(0, 0))
     arrive(1, 1)
     unpack(1, 1)
     rim_pass(3, keep_adjoint)
-    for n in range(2, n_rounds):
-        next_round(n)
+    pl.when(between & jnp.logical_not(turns))(wait_down)
     for c, value in enumerate(strain(3)):
         A[c] = value
     if paired and 0 in RELAYED:
@@ -418,6 +429,11 @@
     packed = jnp.where(lane < 64, spread(-2), spread(2))
     msg[...] = packed.reshape(m_size, e_size, width, 128)
 
+    pl.semaphore_wait(rounds.at[2], 1)
+    if chips > 1:
+        pl.when(is_last)(wait_up)
+        pl.when(is_first)(wait_down)
+
     def peer(oe, om):
         return lax.rem(ev + oe, e_size), lax.rem(me + om, m_size)
 
@@ -442,12 +458,18 @@
 
     for copy in coef_copies:
         copy.wait_recv()
-    coef_copies += [
-        remote(coef_in.at[0], coef_in.at[2], coef_s.at[2], coef_r.at[2],
-               (lax.rem(ev + 1, e_size), me)),
-        remote(coef_in.at[1], coef_in.at[3], coef_s.at[3], coef_r.at[3],
-               (lax.rem(ev + e_size - 1, e_size), me)),
-    ]
+    has_next, has_last = ev < e_size - 1, ev > 0
+
+    def chain_copy(n, step):
+        return pltpu.make_async_remote_copy(
+            src_ref=coef_in.at[n], dst_ref=coef_in.at[2 + n], send_sem=coef_s.at[2 + n],
+            recv_sem=coef_r.at[2 + n], device_id=(lax.rem(ev + step + e_size, e_size), me),
+            device_id_type=MESH,
+        )
+
+    to_next, to_last = chain_copy(0, 1), chain_copy(1, -1)
+    pl.when(has_next)(lambda: to_next.start())
+    pl.when(has_last)(lambda: to_last.start())
     if not direct:
         for copy in a_copies:
             copy.wait_recv()
@@ -470,8 +492,8 @@
     unpack(2, 1)
     rim_pass(0, final)
 
-    for copy in coef_copies[2:]:
-        copy.wait_recv()
+    pl.when(has_last)(lambda: to_next.wait_recv())
+    pl.when(has_next)(lambda: to_last.wait_recv())
     own_coef = pltpu.roll(coef[...], 2, 1)
     left = jnp.where(lin > 0, jnp.where(me > 0, coef_in[0], coef_in[2]), 0.0)
     right = jnp.where(
@@ -522,6 +544,8 @@
             copy.wait_send()
     for copy in coef_copies:
         copy.wait_send()
+    pl.when(has_next)(lambda: to_next.wait_send())
+    pl.when(has_last)(lambda: to_last.wait_send())
 
 
 def write_out(final_vmem, tiles_vmem, final_hbm, tiles_hbm, sems):
@@ -600,7 +624,7 @@
                 pltpu.VMEM(got2, f32),
                 dma((6,)), dma((7,)), dma((3, 2, 3)), dma((3, 2, 3)), dma((4,)), dma((4,)),
                 dma((a_count,)), dma((a_count,)), dma((b_count,)), dma((b_count,)),
-                pltpu.SemaphoreType.REGULAR((max(round_count(m_size, e_size), 1),)),
+                pltpu.SemaphoreType.REGULAR((3,)),
             ],
             compiler_params=pltpu.CompilerParams(collective_id=0, has_side_effects=True),
         )(*args)

time: 18.7 us -> 18.4 us (0.984)
  Pallas kernels: 17.2 us -> 16.9 us
    pallas_call x1, Pallas kernels: 16.5 us -> 16.2 us  [per_device(): pl.pallas_call(functools.partial(kernel, m_size, e_size), out_shape=(pltp...]
where the time goes in v6:
time: 18.4 us; the launch traced here: 18.2 us
  Pallas kernels  16.9 us (92%)
  between operations  1.29 us (7%)
    pallas_call x1, Pallas kernels, per_device(): pl.pallas_call(functools.partial(kernel, m_size, e_size), out_shape=(pltp...  16.2 us
    pallas_call x1, Pallas kernels, per_device(): pl.pallas_call(write_out, out_shape=(pltpu.HBM(line, f32), pltpu.HBM((wid...  0.71 us

profile of v6, /device:TPU:0, one launch (start us, length us, event | category | flops | bytes accessed | tf_op | source)
XLA Modules:
  0.0 18.2 jit_solution(17262098562791456232)
XLA Ops:
  1.3 16.2 %shard_map.104 = (f32[3,128,128]{2,1,0:T(8,128)S(1)}, f32[4,64]{1,0:T(4,128)S(1)}) custom-call(f32[375,1,128]{2,1,0:T(1,128)} %bitcast.6, f32[375,1,128]{2,1,0:T(1,128)} %bitcast.7, f32[125,125]{1,0:T(8,128)} %stiff_hbm.1, f32[64,125]{1,0:T(8,128)} %bitcast.8, f32[1,128]{1,0:T(1,128)} %mat_hbm.1, s32[6,1,128]{2,1,0:T(1,128)} %bitcast.9, s32[1,128]{1,0:T(1,128)} %dest_hbm.1, ...), custom_call_target="tpu_custom_call" | custom-call | tf_op jit(solution)/shard_map/pallas_call | solution.py:595
  17.5 0.7 %shard_map.105 = (f32[375,1,128]{2,1,0:T(1,128)}, f32[4,64]{1,0:T(4,128)}) custom-call(f32[3,128,128]{2,1,0:T(8,128)S(1)} %get-tuple-element.6.final_vmem, f32[4,64]{1,0:T(4,128)S(1)} %get-tuple-element.7.tiles_vmem), custom_call_target="tpu_custom_call" | custom-call | tf_op jit(solution)/shard_map/pallas_call | solution.py:631

commit v7 on v6

--- a/solution.py
+++ b/solution.py
@@ -364,6 +364,7 @@
     own_pass(3)
     own_pass(0)
     pl.when(between)(wait_up)
+    pl.when(turns)(wait_down)
     build_masks(1, lambda relative: (relative == 1) | (relative == m_size - 1))
 
     def keep_adjoint(c, t, value):
@@ -379,7 +380,6 @@
 
     arrive(1, 0)
     unpack(1, 0)
-    pl.when(turns)(wait_down)
     if paired and 0 in RELAYED:
         at_core(1, lambda: arrive(0, 0))
     arrive(1, 1)
@@ -406,7 +406,7 @@
             send_far(2)
         send_near(2)
 
-    ahead = chip < chips // 2
+    ahead = chip == 0
     pl.when(ahead)(send_second)
     elements = F.shape[-1]
     width = smooth_in.shape[1]

time: 18.4 us -> 18.3 us (level)
  no operation moved by 1% of the time
where the time goes in v7:
time: 18.3 us; the launch traced here: 18.2 us
  Pallas kernels  16.9 us (92%)
  between operations  1.29 us (7%)
    pallas_call x1, Pallas kernels, per_device(): pl.pallas_call(functools.partial(kernel, m_size, e_size), out_shape=(pltp...  16.2 us
    pallas_call x1, Pallas kernels, per_device(): pl.pallas_call(write_out, out_shape=(pltpu.HBM(line, f32), pltpu.HBM((wid...  0.71 us

profile of v7, /device:TPU:0, one launch (start us, length us, event | category | flops | bytes accessed | tf_op | source)
XLA Modules:
  0.0 18.2 jit_solution(2227546564565114113)
XLA Ops:
  1.3 16.2 %shard_map.104 = (f32[3,128,128]{2,1,0:T(8,128)S(1)}, f32[4,64]{1,0:T(4,128)S(1)}) custom-call(f32[375,1,128]{2,1,0:T(1,128)} %bitcast.6, f32[375,1,128]{2,1,0:T(1,128)} %bitcast.7, f32[125,125]{1,0:T(8,128)} %stiff_hbm.1, f32[64,125]{1,0:T(8,128)} %bitcast.8, f32[1,128]{1,0:T(1,128)} %mat_hbm.1, s32[6,1,128]{2,1,0:T(1,128)} %bitcast.9, s32[1,128]{1,0:T(1,128)} %dest_hbm.1, ...), custom_call_target="tpu_custom_call" | custom-call | tf_op jit(solution)/shard_map/pallas_call | solution.py:595
  17.5 0.7 %shard_map.105 = (f32[375,1,128]{2,1,0:T(1,128)}, f32[4,64]{1,0:T(4,128)}) custom-call(f32[3,128,128]{2,1,0:T(8,128)S(1)} %get-tuple-element.6.final_vmem, f32[4,64]{1,0:T(4,128)S(1)} %get-tuple-element.7.tiles_vmem), custom_call_target="tpu_custom_call" | custom-call | tf_op jit(solution)/shard_map/pallas_call | solution.py:631

commit v8 on v7

--- a/solution.py
+++ b/solution.py
@@ -80,7 +80,7 @@
     fwd_in, adj_in, stiff_hbm, proj_hbm, mat_hbm, nb_hbm, dest_hbm, count_hbm, smooth_hbm,
     fwd_out, tiles_out,
     stiff_in, proj_in, mat_in, nb_in, dest_in, count_in, smooth_in,
-    F, N, K, A, S, W, M, IDX, RIM, LIVE, send, rim, U, coef, coef_in, msg, mine, part, got, got2,
+    F, N, K, A, S, T, HOT, W, M, IDX, RIM, LIVE, send, rim, U, coef, coef_in, msg, mine, part, got, got2,
     in_s, small_s, rim_s, rim_r, coef_s, coef_r, a_s, a_r, b_s, b_r, rounds,
 ):
     me = lax.axis_index("mesh")
@@ -210,7 +210,11 @@
 
     load_field(1, far_of)
     send_near(1)
-    load_field(0)
+    def forward_of(c):
+        at_core(0, lambda: rim_copy(0, 1, c).start())
+
+    load_field(0, forward_of)
+    at_core(0, lambda: send_near(0))
     coef[...] = jnp.zeros((8, 128), f32)
 
     @pl.when(ev == 0)
@@ -223,7 +227,6 @@
 
     small[0].wait()
     coef[0:4, 0:4] = smooth_in[...]
-    at_core(0, lambda: (send_far(0), send_near(0)))
     coef_copies = [
         remote(coef, coef_in.at[0], coef_s.at[0], coef_r.at[0], (ev, after)),
         remote(coef, coef_in.at[1], coef_s.at[1], coef_r.at[1], (ev, before)),
@@ -378,6 +381,21 @@
         F[c, at, :] = value
         K[line, :] = K[line, :] + value * A[c, line, :]
 
+    elements = F.shape[-1]
+    width = smooth_in.shape[1]
+    scale = math.sqrt(width / elements) / STEPS
+    pad = jnp.zeros((proj_in.shape[0], ROWS - NODES), f32)
+    half = jnp.concatenate([proj_in[...], pad], axis=1)
+    t_hi, t_lo = split(jnp.concatenate([half, half], axis=0))
+    T[...] = jnp.concatenate([t_hi, t_hi, t_lo], axis=1)
+    row = lax.broadcasted_iota(jnp.int32, (total * width, 128), 0)
+    owner = lax.div(row, width)
+    tile = width * (lax.rem(owner, e_size) * m_size + lax.div(owner, e_size)) + lax.rem(row, width)
+    dest = dest_in[...]
+    nt = ((1,), (1,))
+    for at, offset in ((0, -2), (128, 2)):
+        HOT[:, at : at + 128] = jnp.where(tile + offset == dest, 1.0, 0.0).astype(f32).astype(bf16)
+
     arrive(1, 0)
     unpack(1, 0)
     if paired and 0 in RELAYED:
@@ -408,25 +426,14 @@
 
     ahead = chip == 0
     pl.when(ahead)(send_second)
-    elements = F.shape[-1]
-    width = smooth_in.shape[1]
-    scale = math.sqrt(width / elements) / STEPS
-    twin = jnp.concatenate([proj_in[...], proj_in[...]], axis=0)
-    t_hi, t_lo = split(twin)
-    k_hi, k_lo = split(K[0:NODES, :])
-    blocks = (mm(t_hi, k_hi) + (mm(t_hi, k_lo) + mm(t_lo, k_hi))) * scale
-    b_hi, b_lo = split(blocks)
-    row = lax.broadcasted_iota(jnp.int32, (total * width, 128), 0)
-    owner = lax.div(row, width)
-    tile = width * (lax.rem(owner, e_size) * m_size + lax.div(owner, e_size)) + lax.rem(row, width)
-    dest = dest_in[...]
-    nt = ((1,), (1,))
-
-    def spread(offset):
-        hot = jnp.where(tile + offset == dest, 1.0, 0.0).astype(f32).astype(bf16)
-        return mm(hot, b_hi, nt) + mm(hot, b_lo, nt)
-
-    packed = jnp.where(lane < 64, spread(-2), spread(2))
+    k_hi, k_lo = split(K[...])
+    blocks = mm(T[:, 0:256], jnp.concatenate([k_hi, k_lo], axis=0)) + mm(T[:, 256:384], k_hi)
+    blocks = blocks * scale
+    low_half = lax.broadcasted_iota(jnp.int32, (128, 128), 0) < 64
+    b_hi, b_lo = split(jnp.concatenate(
+        [jnp.where(low_half, blocks, 0.0), jnp.where(low_half, 0.0, blocks)], axis=1
+    ))
+    packed = mm(HOT[...], b_hi, nt) + mm(HOT[...], b_lo, nt)
     msg[...] = packed.reshape(m_size, e_size, width, 128)
 
     pl.semaphore_wait(rounds.at[2], 1)
@@ -438,10 +445,20 @@
         return lax.rem(ev + oe, e_size), lax.rem(me + om, m_size)
 
     if direct:
-        offsets = [(oe, om) for oe in list(range(1, e_size)) + [0] for om in range(m_size) if oe or om]
-        for oe, om in offsets:
-            e, m = peer(oe, om)
-            remote(msg.at[m, e], got.at[oe * m_size + om - 1], a_s.at[0], a_r.at[0], (e, m))
+        def to_owner(e, om):
+            m = lax.rem(me + om, m_size)
+            slot = lax.rem(e - ev + e_size, e_size) * m_size + om - 1
+            remote(msg.at[m, e], got.at[slot], a_s.at[0], a_r.at[0], (e, m))
+
+        for e in range(e_size):
+
+            @pl.when(ev != e)
+            def _():
+                for om in range(m_size):
+                    to_owner(jnp.int32(e), om)
+
+        for om in range(1, m_size):
+            to_owner(ev, om)
     else:
         a_copies = [
             remote(msg.at[lax.rem(me + o, m_size)], got.at[pl.ds(e_size * (o - 1), e_size)],
@@ -607,6 +624,8 @@
                 pltpu.VMEM((ROWS, 128), f32),
                 pltpu.VMEM((3, ROWS, 128), f32),
                 pltpu.VMEM((ROWS, ROWS), f32),
+                pltpu.VMEM((128, 3 * ROWS), bf16),
+                pltpu.VMEM((m_size * e_size * width, 256), bf16),
                 pltpu.VMEM((7, ROWS, 128), f32),
                 pltpu.VMEM((2, len(FACE_TILES), 8, 128), f32),
                 pltpu.VMEM((12, 8, 128), jnp.int32),

time: 18.3 us -> 18.3 us (level)
  no operation moved by 1% of the time
where the time goes in v8:
time: 18.3 us; the launch traced here: 18.1 us
  Pallas kernels  16.8 us (92%)
  between operations  1.29 us (7%)
    pallas_call x1, Pallas kernels, per_device(): pl.pallas_call(functools.partial(kernel, m_size, e_size), out_shape=(pltp...  16.1 us
    pallas_call x1, Pallas kernels, per_device(): pl.pallas_call(write_out, out_shape=(pltpu.HBM(line, f32), pltpu.HBM((wid...  0.71 us

profile of v8, /device:TPU:0, one launch (start us, length us, event | category | flops | bytes accessed | tf_op | source)
XLA Modules:
  0.0 18.1 jit_solution(9660929762279394171)
XLA Ops:
  1.3 16.1 %shard_map.104 = (f32[3,128,128]{2,1,0:T(8,128)S(1)}, f32[4,64]{1,0:T(4,128)S(1)}) custom-call(f32[375,1,128]{2,1,0:T(1,128)} %bitcast.6, f32[375,1,128]{2,1,0:T(1,128)} %bitcast.7, f32[125,125]{1,0:T(8,128)} %stiff_hbm.1, f32[64,125]{1,0:T(8,128)} %bitcast.8, f32[1,128]{1,0:T(1,128)} %mat_hbm.1, s32[6,1,128]{2,1,0:T(1,128)} %bitcast.9, s32[1,128]{1,0:T(1,128)} %dest_hbm.1, ...), custom_call_target="tpu_custom_call" | custom-call | tf_op jit(solution)/shard_map/pallas_call | solution.py:612
  17.4 0.7 %shard_map.105 = (f32[375,1,128]{2,1,0:T(1,128)}, f32[4,64]{1,0:T(4,128)}) custom-call(f32[3,128,128]{2,1,0:T(8,128)S(1)} %get-tuple-element.6.final_vmem, f32[4,64]{1,0:T(4,128)S(1)} %get-tuple-element.7.tiles_vmem), custom_call_target="tpu_custom_call" | custom-call | tf_op jit(solution)/shard_map/pallas_call | solution.py:650

commit v9 on v8

--- a/solution.py
+++ b/solution.py
@@ -16,7 +16,7 @@
 ROWS = 128
 NODES = 125
 SHIFT = (100, -100, 20, -20, 4, -4)
-RELAYED = (0,)
+RELAYED = (0, 1)
 MESH = pl.DeviceIdType.MESH
 f32 = jnp.float32
 bf16 = jnp.bfloat16
@@ -206,10 +206,21 @@
     def far_of(c):
         if c == 0:
             pl.semaphore_wait(barrier, near_count + (m_size - 1))
-        rim_copy(1, 1, c).start()
+
+        def leave():
+            rim_copy(1, 1, c).start()
+
+        if paired and 1 in RELAYED:
+            at_core(0, leave)
+            at_core(1, lambda: rim_copy(1, 0, c).start())
+        else:
+            leave()
 
     load_field(1, far_of)
-    send_near(1)
+    if paired and 1 in RELAYED:
+        at_core(0, lambda: send_near(1))
+    else:
+        send_near(1)
     def forward_of(c):
         at_core(0, lambda: rim_copy(0, 1, c).start())
 

time: 18.3 us -> 18.2 us (level)
  no operation moved by 1% of the time
where the time goes in v9:
time: 18.2 us; the launch traced here: 18 us
  Pallas kernels  16.7 us (92%)
  between operations  1.29 us (7%)
    pallas_call x1, Pallas kernels, per_device(): pl.pallas_call(functools.partial(kernel, m_size, e_size), out_shape=(pltp...  16 us
    pallas_call x1, Pallas kernels, per_device(): pl.pallas_call(write_out, out_shape=(pltpu.HBM(line, f32), pltpu.HBM((wid...  0.71 us

profile of v9, /device:TPU:0, one launch (start us, length us, event | category | flops | bytes accessed | tf_op | source)
XLA Modules:
  0.0 18.0 jit_solution(7116622923621394839)
XLA Ops:
  1.3 16.0 %shard_map.104 = (f32[3,128,128]{2,1,0:T(8,128)S(1)}, f32[4,64]{1,0:T(4,128)S(1)}) custom-call(f32[375,1,128]{2,1,0:T(1,128)} %bitcast.6, f32[375,1,128]{2,1,0:T(1,128)} %bitcast.7, f32[125,125]{1,0:T(8,128)} %stiff_hbm.1, f32[64,125]{1,0:T(8,128)} %bitcast.8, f32[1,128]{1,0:T(1,128)} %mat_hbm.1, s32[6,1,128]{2,1,0:T(1,128)} %bitcast.9, s32[1,128]{1,0:T(1,128)} %dest_hbm.1, ...), custom_call_target="tpu_custom_call" | custom-call | tf_op jit(solution)/shard_map/pallas_call | solution.py:623
  17.3 0.7 %shard_map.105 = (f32[375,1,128]{2,1,0:T(1,128)}, f32[4,64]{1,0:T(4,128)}) custom-call(f32[3,128,128]{2,1,0:T(8,128)S(1)} %get-tuple-element.6.final_vmem, f32[4,64]{1,0:T(4,128)S(1)} %get-tuple-element.7.tiles_vmem), custom_call_target="tpu_custom_call" | custom-call | tf_op jit(solution)/shard_map/pallas_call | solution.py:661
